TPU v7x, 32 devices: a whole 2x2x4 slice. The times are simulated.
32 devices in a mesh: ctx: 8 (over z, y), fsdp: 4 (over x, core).
Axes of the slice: x: 2, y: 2, z: 4, core: 2. Of those that a mesh axis runs over, the one named last changes fastest.
Arguments:
- block_input: float32 [4, 1024, 960], P('fsdp', 'ctx'), may hold values from -20 to 20
- pair_of_device: int32 [8], replicated, may hold values from 0 to 7, each once
- query_weight: bfloat16 [1, 960, 960], P(None, 'fsdp'), may hold values from -0.1875 to 0.1875
- key_weight: bfloat16 [1, 960, 320], P(None, 'fsdp'), may hold values from -0.1875 to 0.1875
- value_matrix: bfloat16 [1, 960, 320], P(None, 'fsdp'), may hold values from -0.1875 to 0.1875
- output_weight: bfloat16 [1, 960, 960], P(None, None, 'fsdp'), may hold values from -0.75 to 0.75
- gate_weight: bfloat16 [1, 960, 2560], P(None, 'fsdp'), may hold values from -0.1875 to 0.1875
- up_weight: bfloat16 [1, 960, 2560], P(None, 'fsdp'), may hold values from -0.1875 to 0.1875
- down_weight: bfloat16 [1, 2560, 960], P(None, None, 'fsdp'), may hold values from -0.125 to 0.125
- attention_gain: float32 [1, 960], replicated, may hold values from 0.5 to 1.5
- feedforward_gain: float32 [1, 960], replicated, may hold values from 0.5 to 1.5
- output_cotangent: float32 [4, 1024, 960], P('fsdp', 'ctx'), may hold values from -6 to 6
Outputs:
- block_output: float32 [4, 1024, 960], P('fsdp', 'ctx')
- input_grad: float32 [4, 1024, 960], P('fsdp', 'ctx')
- query_weight_grad: float32 [1, 960, 960], P(None, 'fsdp', 'ctx')
- key_weight_grad: float32 [1, 960, 320], P(None, 'fsdp', 'ctx')
- value_weight_grad: float32 [1, 960, 320], P(None, 'fsdp', 'ctx')
- output_weight_grad: float32 [1, 960, 960], P(None, 'ctx', 'fsdp')
- gate_weight_grad: float32 [1, 960, 2560], P(None, 'fsdp', 'ctx')
- up_weight_grad: float32 [1, 960, 2560], P(None, 'fsdp', 'ctx')
- down_weight_grad: float32 [1, 2560, 960], P(None, 'ctx', 'fsdp')
- attention_gain_grad: float32 [1, 960], replicated
- feedforward_gain_grad: float32 [1, 960], replicated
All inputs are finite; a program needn't handle non-finite values.
Results may differ from a plain program's by a relative error of at most 0.024.
Values may be sent and summed in bfloat16 or wider, within the bound.
No kernel may reach another device: no remote copies, remote signals or barrier semaphores. Data moves between devices by JAX's collectives and lax.ppermute only.
A program may use at most 192 MiB of HBM per device.

v0:
```python
import math

import jax
import jax.numpy as jnp
from jax import lax
from jax.experimental import pallas as pl
from jax.experimental.pallas import tpu as pltpu
from jax.sharding import PartitionSpec as P

QUERY_HEADS = 15
KEY_HEADS = 5
HEAD_SIZE = 64
GROUP = QUERY_HEADS // KEY_HEADS
QUERY_WIDTH = QUERY_HEADS * HEAD_SIZE
KEY_WIDTH = KEY_HEADS * HEAD_SIZE
EPSILON = 1e-05
THETA = 100000.0
SCALE = 1.0 / math.sqrt(HEAD_SIZE)
F32 = jnp.float32
BF16 = jnp.bfloat16


def dot_nn(left, right):
    return lax.dot_general(left, right, (((1,), (0,)), ((), ())), preferred_element_type=F32)


def dot_nt(left, right):
    return lax.dot_general(left, right, (((1,), (1,)), ((), ())), preferred_element_type=F32)


def dot_tn(left, right):
    return lax.dot_general(left, right, (((0,), (0,)), ((), ())), preferred_element_type=F32)


def swap(value, axis, bit):
    size = lax.axis_size(axis)
    return lax.ppermute(value, axis, [(i, i ^ bit) for i in range(size)])


def bits_of(axis):
    size = lax.axis_size(axis)
    result = []
    bit = 1
    while bit < size:
        result.append(bit)
        bit *= 2
    return result


def gather_blocks(value, axis):
    blocks = {0: value}
    order = [0]
    for bit in reversed(bits_of(axis)):
        for j in list(order):
            blocks[j ^ bit] = swap(blocks[j], axis, bit)
            order.append(j ^ bit)
    return [blocks[j] for j in range(len(order))]


def gather_levels(value, axis, beside):
    count = lax.axis_size(axis)
    blocks = {0: value}
    level = [0]
    extras = []
    while len(blocks) < count:
        width = bin(level[0]).count("1") + 1
        token = blocks[level[-1]]
        level = [j for j in range(count) if bin(j).count("1") == width]
        for j in sorted(level, reverse=True):
            blocks[j] = swap(blocks[j & (j - 1)], axis, j & -j)
        extra = beside[width - 1](token) if width <= len(beside) else ()
        gated, extra = lax.optimization_barrier((tuple(blocks[j] for j in level), extra))
        blocks.update(zip(level, gated))
        extras.append(extra)
    return [blocks[j] for j in range(count)], extras


def exchange_blocks(blocks, axis):
    return [blocks[0]] + [swap(blocks[j], axis, j) for j in range(1, len(blocks))]


def split_side(value, own, k):
    pairs = value.reshape(value.shape[0] // 2, 2, *value.shape[1:])
    side = (own >> k) & 1
    kept = lax.dynamic_index_in_dim(pairs, side, 1, keepdims=False)
    return kept, lax.dynamic_index_in_dim(pairs, 1 - side, 1, keepdims=False)


def half_step(kept, received):
    total = (kept.astype(F32) + received.astype(F32)).astype(BF16)
    pairs = total.reshape(total.shape[0] // 2, 2, *total.shape[1:])
    return pairs[:, 0], pairs[:, 1]


class Hbm:
    def __init__(self, value, index=()):
        self.value, self.index = value, index


def hbm(values):
    return [Hbm(v) for v in values]


class LateInput:
    def __init__(self, buffer, copy):
        self.buffer, self.copy, self.waiting = buffer, copy, True

    def ready(self):
        if self.waiting:
            self.copy.wait()
            self.waiting = False

    @property
    def shape(self):
        return self.buffer.shape

    def __getitem__(self, index):
        self.ready()
        return self.buffer[index]


class LateOutput:
    def __init__(self, buffer, copy):
        self.buffer, self.copy, self.started = buffer, copy, False

    def flush(self):
        if not self.started:
            self.copy.start()
            self.started = True

    def __getitem__(self, index):
        return self.buffer[index]

    def __setitem__(self, index, value):
        self.buffer[index] = value


def launch(body, outs, scalars, arrays, scratch=()):
    late_in = [isinstance(a, Hbm) for a in arrays]
    values = [a.value if isinstance(a, Hbm) else a for a in arrays]
    picks = [a.index if isinstance(a, Hbm) else () for a in arrays]
    late_out = [len(o) == 3 for o in outs]
    count_in, count_out = sum(late_in), sum(late_out)
    vmem = pl.BlockSpec(memory_space=pltpu.VMEM)
    away = pl.BlockSpec(memory_space=pl.ANY)
    buffers = [
        pltpu.VMEM(v.shape[len(p) :], v.dtype) for v, p, late in zip(values, picks, late_in) if late
    ]
    buffers += [pltpu.VMEM(o[0], o[1]) for o, late in zip(outs, late_out) if late]
    if buffers:
        buffers.append(pltpu.SemaphoreType.DMA((count_in + count_out,)))

    def wrapped(*refs):
        at = len(scalars)
        items = list(refs[:at])
        ins = refs[at : at + len(values)]
        at += len(values)
        results = refs[at : at + len(outs)]
        at += len(outs)
        own_scratch = refs[at : at + len(scratch)]
        spare = list(refs[at + len(scratch) :])
        late_ins, late_outs = [], []
        slot = 0
        for ref, pick, late in zip(ins, picks, late_in):
            if late:
                source = ref.at[pick] if pick else ref
                copy = pltpu.make_async_copy(source, spare[slot], spare[-1].at[slot])
                copy.start()
                late_ins.append(LateInput(spare[slot], copy))
                items.append(late_ins[-1])
                slot += 1
            else:
                items.append(ref)
        for ref, late in zip(results, late_out):
            if late:
                copy = pltpu.make_async_copy(spare[slot], ref, spare[-1].at[slot])
                late_outs.append(LateOutput(spare[slot], copy))
                items.append(late_outs[-1])
                slot += 1
            else:
                items.append(ref)
        body(*items, *own_scratch)
        for item in late_ins:
            item.ready()
        for item in late_outs:
            item.flush()
        for item in late_outs:
            item.copy.wait()

    return pl.pallas_call(
        wrapped,
        out_shape=[jax.ShapeDtypeStruct(o[0], o[1]) for o in outs],
        in_specs=[pl.BlockSpec(memory_space=pltpu.SMEM) for _ in scalars]
        + [away if late else vmem for late in late_in],
        out_specs=[away if late else vmem for late in late_out],
        scratch_shapes=list(scratch) + buffers,
        compiler_params=pltpu.CompilerParams(vmem_limit_bytes=60 * 1024 * 1024),
    )(*scalars, *values)


def after(value, *others):
    return lax.optimization_barrier((value, *others))[0]


def rotated(values, cosine, sine):
    width = values.shape[-1]
    lane = lax.broadcasted_iota(jnp.int32, values.shape, 1)
    ahead = pltpu.roll(values, width - HEAD_SIZE // 2, 1)
    behind = pltpu.roll(values, HEAD_SIZE // 2, 1)
    other = jnp.where((lane % HEAD_SIZE) < HEAD_SIZE // 2, ahead, behind)
    repeat = width // cosine.shape[-1]
    return values * jnp.tile(cosine, (1, repeat)) + other * jnp.tile(sine, (1, repeat))


def norm_of(hidden):
    factor = lax.rsqrt(jnp.mean(hidden * hidden, axis=-1, keepdims=True) + EPSILON)
    return hidden * factor, factor


def prepare_body(parts):
    def body(*refs):
        hidden_ref, cotangent_ref, gain_ref, query_ref, key_ref, value_ref = refs[:6]
        weight_ref, input_ref, feed_ref, rows_ref = refs[6:]
        weight_ref[...] = jnp.concatenate(
            [query_ref[...], key_ref[...].T, value_ref[...].T], axis=1
        )
        weight_ref.flush()
        hidden = hidden_ref[...].T
        cotangent = cotangent_ref[...].T
        rows_ref[0] = hidden
        rows_ref[1] = cotangent
        normed, _ = norm_of(hidden)
        attend = (normed * gain_ref[...]).astype(BF16)
        feed = cotangent.astype(BF16)
        block = attend.shape[-1] // parts
        for b in range(parts):
            input_ref[b, :, :block] = attend[:, b * block : (b + 1) * block]
            feed_ref[b, :, :block] = feed[:, b * block : (b + 1) * block]

    return body


def deal_body(parts, count):
    def body(*refs):
        own = refs[0][0]
        weight_refs = refs[1:4]
        own_ref, near_ref, far_ref, scratch = refs[4:]
        for m in range(3):
            values = weight_refs[m][...]
            chunk = values.shape[1] // count
            share = chunk // parts
            for g in range(parts):
                scratch[g] = jnp.concatenate(
                    [
                        values[:, c * chunk + g * share : c * chunk + (g + 1) * share]
                        for c in range(count)
                    ],
                    axis=1,
                )
            far_ref[0, m] = scratch[own ^ 2]
            far_ref[1, m] = scratch[own ^ 3]
            own_ref[m] = scratch[own]
            near_ref[m] = scratch[own ^ 1]

    return body


def project_body(parts, block):
    def body(*refs):
        own = refs[0][0]
        input_ref, cosine_ref, sine_ref = refs[1:4]
        weight_refs = refs[4 : 4 + parts]
        query_ref, pair_ref = refs[4 + parts :]
        result = None
        for j in range(parts):
            term = dot_nn(input_ref[own ^ j][:, :block], weight_refs[j][...])
            result = term if result is None else result + term
        both = rotated(result[:, : QUERY_WIDTH + KEY_WIDTH], cosine_ref[...], sine_ref[...])
        both = both.astype(BF16)
        query_ref[...] = both[:, :QUERY_WIDTH]
        pair_ref[:, :KEY_WIDTH] = both[:, QUERY_WIDTH:]
        pair_ref[:, KEY_WIDTH:] = result[:, QUERY_WIDTH + KEY_WIDTH :].astype(BF16)

    return body


def stack_group(values, head, half):
    pieces = []
    for start in (half, 0):
        for g in range(GROUP):
            lane = (head * GROUP + g) * HEAD_SIZE
            pieces.append(values[start : start + half, lane : lane + HEAD_SIZE])
    return jnp.concatenate(pieces, axis=0)


def unstack_groups(groups, half):
    late = [g[i * half : (i + 1) * half] for g in groups for i in range(GROUP)]
    early = [g[(GROUP + i) * half : (GROUP + i + 1) * half] for g in groups for i in range(GROUP)]
    return jnp.concatenate(
        [jnp.concatenate(early, axis=1), jnp.concatenate(late, axis=1)], axis=0
    )


def split_keys(pair_refs, early_scratch, late_scratch, half):
    for j, pair_ref in enumerate(pair_refs):
        early_scratch[j * half : (j + 1) * half, :] = pair_ref[:half, :]
        late_scratch[j * half : (j + 1) * half, :] = pair_ref[half:, :]


def attend_body(parts, count, half):
    wide = GROUP * half

    def body(*refs):
        own = refs[0][0]
        query_ref, early_pos, late_pos, row_pos, rows_ref, gain_ref = refs[1:7]
        pair_refs = refs[7 : 7 + count]
        output_refs = refs[7 + count : 7 + count + parts]
        mixed_ref, total_ref, middle_ref, feed_ref = refs[7 + count + parts : 11 + count + parts]
        early_scratch, late_scratch, block_scratch = refs[11 + count + parts :]
        split_keys(pair_refs, early_scratch, late_scratch, half)
        query = query_ref[...] * SCALE
        visible_early = early_pos[...] <= row_pos[...]
        visible_late = late_pos[...] <= row_pos[:, :wide]
        groups = []
        for h in range(KEY_HEADS):
            lane = h * HEAD_SIZE
            rows = stack_group(query, h, half)
            key_early = early_scratch[:, lane : lane + HEAD_SIZE]
            key_late = late_scratch[:, lane : lane + HEAD_SIZE]
            value_early = early_scratch[:, KEY_WIDTH + lane : KEY_WIDTH + lane + HEAD_SIZE]
            value_late = late_scratch[:, KEY_WIDTH + lane : KEY_WIDTH + lane + HEAD_SIZE]
            score_early = jnp.where(visible_early, dot_nt(key_early, rows), -1e30)
            score_late = jnp.where(visible_late, dot_nt(key_late, rows[:wide]), -1e30)
            high_early = jnp.max(score_early, axis=0, keepdims=True)
            high_late = jnp.max(score_late, axis=0, keepdims=True)
            high_late = jnp.maximum(high_early[:, :wide], high_late)
            high = jnp.concatenate([high_late, high_early[:, wide:]], axis=1)
            raised_early = jnp.exp(score_early - high)
            raised_late = jnp.exp(score_late - high_late)
            sum_early = jnp.sum(raised_early, axis=0, keepdims=True)
            sum_late = sum_early[:, :wide] + jnp.sum(raised_late, axis=0, keepdims=True)
            total = jnp.concatenate([sum_late, sum_early[:, wide:]], axis=1)
            inverse = 1.0 / total
            mixed_early = dot_tn(value_early, (raised_early * inverse).astype(BF16))
            mixed_late = dot_tn(value_late, (raised_late * inverse[:, :wide]).astype(BF16))
            joined = jnp.concatenate(
                [mixed_early[:, :wide] + mixed_late, mixed_early[:, wide:]], axis=1
            )
            groups.append(joined.T)
            total_ref[h : h + 1, :] = high + jnp.log(total)
        mixed = unstack_groups(groups, half).astype(BF16)
        mixed_ref[...] = mixed
        for j in range(parts):
            block_scratch[own ^ j] = dot_nn(mixed, output_refs[j][...])
        middle = rows_ref[0] + jnp.concatenate(
            [block_scratch[b] for b in range(parts)], axis=1
        )
        middle_ref[...] = middle
        normed, _ = norm_of(middle)
        feed = (normed * gain_ref[...]).astype(BF16)
        block = feed.shape[-1] // parts
        for b in range(parts):
            feed_ref[b, :, :block] = feed[:, b * block : (b + 1) * block]

    return body


def row_blocks(refs, block, *index):
    return jnp.concatenate([r[index] for r in refs], axis=0)[:, :block]


def put_rows(kept_ref, sent_ref, block, values, rows):
    for i in range(values.shape[0] // rows):
        target = sent_ref if i % 2 else kept_ref
        target[i // 2, block, :, : values.shape[1]] = values[i * rows : (i + 1) * rows]


def down_weights(values):
    return [Hbm(v, (0, 2) if v.ndim == 4 else (2,)) for v in values]


def feed_weight(refs, j, m):
    return refs[2][0, m] if j == 2 else refs[j][m]


def feed_body(parts, block):
    def body(*refs):
        own = refs[0][0]
        input_refs = refs[1 : 1 + parts]
        feed_refs = refs[1 + parts : 1 + 2 * parts]
        weight_refs = refs[1 + 2 * parts : 1 + 3 * parts]
        kept_ref, sent_ref, hidden_ref, gate_ref, up_ref = refs[1 + 3 * parts :]
        rows = input_refs[0].shape[1]
        gate = up = units = None
        for j in range(parts):
            rows_in = row_blocks(input_refs, block, own ^ j)
            feed = row_blocks(feed_refs, block, own ^ j)
            terms = [
                dot_nn(rows_in, feed_weight(weight_refs, j, 0)),
                dot_nn(rows_in, feed_weight(weight_refs, j, 1)),
                dot_nn(feed, feed_weight(weight_refs, j, 2)),
            ]
            if gate is None:
                gate, up, units = terms
            else:
                gate, up, units = gate + terms[0], up + terms[1], units + terms[2]
        sigmoid = 1.0 / (1.0 + jnp.exp(-gate))
        silu = gate * sigmoid
        hidden_ref[...] = (silu * up).astype(BF16)
        grad_up = (units * silu).astype(BF16)
        grad_gate = (units * up * sigmoid * (1.0 + gate * (1.0 - sigmoid))).astype(BF16)
        gate_ref[...] = grad_gate
        up_ref[...] = grad_up
        for j in range(parts):
            back = dot_nt(grad_gate, feed_weight(weight_refs, j, 0))
            back = back + dot_nt(grad_up, feed_weight(weight_refs, j, 1))
            put_rows(kept_ref, sent_ref, own ^ j, back.astype(BF16), rows)

    return body


def put_units(kept_ref, sent_ref, first, at, values, count):
    share = values.shape[0] // count
    for c in range(0, count, 2):
        even = values[c * share : (c + 1) * share]
        odd = values[(c + 1) * share : (c + 2) * share]
        kept_ref[c // 2, at : at + share] = jnp.where(first, even, odd).astype(BF16)
        sent_ref[c // 2, at : at + share] = jnp.where(first, odd, even).astype(BF16)


def feed_grads_body(parts, count, block):
    def body(*refs):
        own = refs[0][0]
        first = refs[1][0] == 0
        input_refs = refs[2 : 2 + parts]
        feed_refs = refs[2 + parts : 2 + 2 * parts]
        left_refs = refs[2 + 2 * parts : 5 + 2 * parts]
        grad_refs = refs[5 + 2 * parts :]
        share = left_refs[0].shape[1] // count
        for m in range(3):
            kept_ref, sent_ref = grad_refs[2 * m : 2 * m + 2]
            for j in range(parts):
                rows_in = row_blocks(input_refs if m else feed_refs, block, own ^ j)
                grads = dot_tn(left_refs[m][...], rows_in)
                put_units(kept_ref, sent_ref, first, j * share, grads, count)
            sent_ref.flush()
            kept_ref.flush()

    return body


def feed_out_body(parts, rows):
    def body(*refs):
        own = refs[0][0]
        weight_refs = refs[1 : 1 + parts]
        hidden_ref, kept_out, sent_out = refs[1 + parts :]
        for j in range(parts):
            out = dot_nt(hidden_ref[...], weight_refs[j][...]).astype(BF16)
            put_rows(kept_out, sent_out, own ^ j, out, rows)

    return body


def gate_up_grads_body(parts, count, block):
    def body(*refs):
        own = refs[0][0]
        first = refs[1][0] == 0
        input_refs = refs[2 : 2 + parts]
        left_refs = refs[2 + parts : 4 + parts]
        grad_refs = refs[4 + parts :]
        for m in range(2):
            for j in range(parts):
                grads = dot_tn(left_refs[m][...], row_blocks(input_refs, block, own ^ j))
                put_units(grad_refs[2 * m], grad_refs[2 * m + 1], first, j, grads, count)
            grad_refs[2 * m + 1].flush()
            grad_refs[2 * m].flush()

    return body


def joined_blocks(kept_ref, received_ref, passed_ref, parts, block):
    return jnp.concatenate(
        [
            (
                kept_ref[0, b].astype(F32)
                + received_ref[0, b].astype(F32)
                + passed_ref[b].astype(F32)
            )[:, :block]
            for b in range(parts)
        ],
        axis=1,
    )


def back_body(parts, count, half, block):
    wide = GROUP * half

    def body(*refs):
        own = refs[0][0]
        (
            kept_ref,
            received_ref,
            passed_ref,
            middle_ref,
            gain_ref,
            rows_ref,
            mixed_ref,
            query_ref,
            total_ref,
            early_pos,
            late_pos,
            row_pos,
            cosine_ref,
            sine_ref,
        ) = refs[1:15]
        pair_refs = refs[15 : 15 + count]
        output_refs = refs[15 + count : 15 + count + parts]
        at = 15 + count + parts
        grad_middle_ref, pack_ref, gain_grad_ref = refs[at : at + 3]
        grad_pair_refs = refs[at + 3 : at + 5]
        early_scratch, late_scratch = refs[at + 5 :]
        split_keys(pair_refs, early_scratch, late_scratch, half)
        normed, factor = norm_of(middle_ref[...])
        grad = joined_blocks(kept_ref, received_ref, passed_ref, parts, block)
        gain_grad_ref[...] = jnp.sum(grad * normed, axis=0, keepdims=True)
        scaled = grad * gain_ref[...]
        grad_middle = rows_ref[1] + factor * (
            scaled - normed * jnp.mean(scaled * normed, axis=-1, keepdims=True)
        )
        grad_middle_ref[...] = grad_middle
        mixed_in = grad_middle.astype(BF16)
        for b in range(parts):
            pack_ref[1, b, :, :block] = mixed_ref[:, b * block : (b + 1) * block]
            pack_ref[2, b, :, :block] = mixed_in[:, b * block : (b + 1) * block]
        mixed_grad = None
        for j in range(parts):
            term = dot_nt(pack_ref[2, own ^ j][:, :block], output_refs[j][...])
            mixed_grad = term if mixed_grad is None else mixed_grad + term
        mixed_grad = mixed_grad.astype(BF16)
        product = mixed_grad.astype(F32) * mixed_ref[...].astype(F32)
        query = query_ref[...] * SCALE
        visible_early = early_pos[...] <= row_pos[...]
        visible_late = late_pos[...] <= row_pos[:, :wide]
        groups = []
        grads_early = [[], []]
        grads_late = [[], []]
        for h in range(KEY_HEADS):
            lane = h * HEAD_SIZE
            rows = stack_group(query, h, half)
            outer = stack_group(mixed_grad, h, half)
            delta = jnp.sum(stack_group(product, h, half).T, axis=0, keepdims=True)
            log_total = total_ref[h : h + 1, :]
            key_early = early_scratch[:, lane : lane + HEAD_SIZE]
            key_late = late_scratch[:, lane : lane + HEAD_SIZE]
            value_early = early_scratch[:, KEY_WIDTH + lane : KEY_WIDTH + lane + HEAD_SIZE]
            value_late = late_scratch[:, KEY_WIDTH + lane : KEY_WIDTH + lane + HEAD_SIZE]
            probs = jnp.where(visible_early, jnp.exp(dot_nt(key_early, rows) - log_total), 0.0)
            score_grad = (probs * (dot_nt(value_early, outer) - delta)).astype(BF16)
            grads_early[1].append(dot_nn(probs.astype(BF16), outer))
            grads_early[0].append(dot_nn(score_grad, rows))
            query_early = dot_tn(key_early, score_grad)
            probs = jnp.where(
                visible_late, jnp.exp(dot_nt(key_late, rows[:wide]) - log_total[:, :wide]), 0.0
            )
            score_grad = (probs * (dot_nt(value_late, outer[:wide]) - delta[:, :wide])).astype(BF16)
            grads_late[1].append(dot_nn(probs.astype(BF16), outer[:wide]))
            grads_late[0].append(dot_nn(score_grad, rows[:wide]))
            query_late = dot_tn(key_late, score_grad)
            joined = jnp.concatenate(
                [query_early[:, :wide] + query_late, query_early[:, wide:]], axis=1
            )
            groups.append(joined.T)
        grad_query = unstack_groups(groups, half) * SCALE
        padded = jnp.concatenate([grad_query, jnp.zeros_like(grad_query[:, :HEAD_SIZE])], axis=1)
        padded = rotated(padded, cosine_ref[...], -sine_ref[...]).astype(BF16)
        for b in range(parts):
            pack_ref[0, b, :, :block] = padded[:, b * block : (b + 1) * block]
        pair_early = jnp.concatenate(grads_early[0] + grads_early[1], axis=1).astype(BF16)
        pair_late = jnp.concatenate(grads_late[0] + grads_late[1], axis=1).astype(BF16)
        for j in range(count):
            grad_pair_refs[j % 2][j // 2, :half, :] = pair_early[j * half : (j + 1) * half]
            grad_pair_refs[j % 2][j // 2, half:, :] = pair_late[j * half : (j + 1) * half]

    return body


def attention_grads_body(parts, count, block):
    def body(*refs):
        own = refs[0][0]
        first = refs[1][0] == 0
        pack_refs = refs[2 : 2 + parts]
        input_refs = refs[2 + parts : 2 + 2 * parts]
        kept_ref, sent_ref = refs[2 + 2 * parts :]
        inputs = row_blocks(input_refs, block, own)
        mixed_in = row_blocks(pack_refs, block, 2, own)
        grads = [
            jnp.concatenate(
                [dot_tn(row_blocks(pack_refs, block, m, b), right) for b in range(parts)], axis=0
            )
            for m, right in ((0, inputs), (1, mixed_in))
        ]
        put_groups(kept_ref, sent_ref, first, 0, grads, count)

    return body


def put_groups(kept_ref, sent_ref, first, at, grads, count):
    def rows_of(c):
        pieces = []
        for values in grads:
            rows = values.shape[0] // count
            pieces.append(values[c * rows : (c + 1) * rows])
        return jnp.concatenate(pieces, axis=0)

    for c in range(0, count, 2):
        even, odd = rows_of(c), rows_of(c + 1)
        stop = at + even.shape[0]
        kept_ref[c // 2, at:stop] = jnp.where(first, even, odd).astype(BF16)
        sent_ref[c // 2, at:stop] = jnp.where(first, odd, even).astype(BF16)


def output_body(parts, block):
    def body(middle_ref, kept_ref, received_ref, passed_ref, out_ref):
        out = middle_ref[...] + joined_blocks(kept_ref, received_ref, passed_ref, parts, block)
        out_ref[...] = out.T

    return body


def input_grad_body(parts, block):
    def body(*refs):
        own = refs[0][0]
        pair_kept, pair_received, cosine_ref, sine_ref, pack_ref, rows_ref, gain_ref = refs[1:8]
        middle_ref = refs[8]
        weight_refs = refs[9 : 9 + parts]
        pair_ref, grad_ref, gain_grad_ref, block_scratch = refs[9 + parts :]
        pair = pair_kept[0].astype(F32) + pair_received[0].astype(F32)
        turned = rotated(pair, cosine_ref[...], -sine_ref[...])
        pair = jnp.concatenate([turned[:, :KEY_WIDTH], pair[:, KEY_WIDTH:]], axis=1).astype(BF16)
        pair_ref[...] = pair
        grads = [pack_ref[0, b][:, :block] for b in range(parts)] + [pair]
        grads = jnp.concatenate(grads, axis=1)
        for j in range(parts):
            block_scratch[own ^ j] = dot_nt(grads, weight_refs[j][...])
        grad = jnp.concatenate([block_scratch[b] for b in range(parts)], axis=1)
        normed, factor = norm_of(rows_ref[0])
        gain_grad_ref[...] = jnp.sum(grad * normed, axis=0, keepdims=True)
        scaled = grad * gain_ref[...]
        result = middle_ref[...] + factor * (
            scaled - normed * jnp.mean(scaled * normed, axis=-1, keepdims=True)
        )
        grad_ref[...] = result.T

    return body


def pair_grads_body(parts, count, block):
    def body(*refs):
        own = refs[0][0]
        first = refs[1][0] == 0
        pair_refs = refs[2 : 2 + parts]
        acts_refs = refs[2 + parts : 2 + 2 * parts]
        kept_ref, sent_ref = refs[2 + 2 * parts :]
        pairs = jnp.concatenate([r[...] for r in pair_refs], axis=0)
        grads = dot_tn(pairs, row_blocks(acts_refs, block, own))
        put_groups(kept_ref, sent_ref, first, 0, [grads[:KEY_WIDTH], grads[KEY_WIDTH:]], count)

    return body


def shards(
    block_input,
    pair_of_device,
    query_weight,
    key_weight,
    value_matrix,
    output_weight,
    gate_weight,
    up_weight,
    down_weight,
    attention_gain,
    feedforward_gain,
    output_cotangent,
):
    hidden = block_input[0]
    cotangent = output_cotangent[0]
    rows, width = hidden.shape
    half = rows // 2
    count = lax.axis_size("ctx")
    parts = lax.axis_size("fsdp")
    own_ctx = lax.axis_index("ctx")
    own = lax.axis_index("fsdp")
    block = width // parts
    padded = -(-block // 128) * 128
    units = down_weight.shape[1]
    share = units // (count * parts)
    own_scalar = own.astype(jnp.int32).reshape(1)

    device_ids = jnp.arange(count, dtype=jnp.int32)
    relative = own_ctx.astype(jnp.int32) ^ device_ids
    pairs = jnp.sum(
        jnp.where(relative[:, None] == device_ids[None, :], pair_of_device[None, :], 0), axis=1
    )
    within = jnp.arange(half, dtype=jnp.int32)
    early_pos = (pairs[:, None] * half + within[None, :]).reshape(-1, 1)
    late_pos = ((2 * count - 1 - pairs)[:, None] * half + within[None, :]).reshape(-1, 1)
    own_early = pairs[0] * half + within
    own_late = (2 * count - 1 - pairs[0]) * half + within
    row_pos = jnp.concatenate([own_late] * GROUP + [own_early] * GROUP)[None, :]
    half_head = HEAD_SIZE // 2
    frequency = jnp.exp(
        jnp.arange(half_head, dtype=F32) * (-2.0 * math.log(THETA) / HEAD_SIZE)
    )
    positions = jnp.concatenate([own_early, own_late])
    angles = positions.astype(F32)[:, None] * frequency[None, :]
    cosine, sine = jnp.cos(angles), jnp.sin(angles)
    cosine = jnp.concatenate([cosine] * 4, axis=1)
    sine = jnp.concatenate([-sine, sine] * 2, axis=1)

    side_scalar = (own_ctx & 1).astype(jnp.int32).reshape(1)
    hidden_count = count * share

    weight_pack, attend_input, grad_feed, both_rows = launch(
        prepare_body(parts),
        [
            ((block, QUERY_WIDTH + 2 * KEY_WIDTH), BF16, True),
            ((parts, rows, padded), BF16),
            ((parts, rows, padded), BF16),
            ((2, rows, width), F32),
        ],
        [],
        [
            hidden.T,
            cotangent.T,
            attention_gain,
            query_weight[0],
            key_weight[0].T,
            value_matrix[0].T,
        ],
    )
    weight_far = swap(weight_pack, "fsdp", 2)
    weight_near = swap(weight_pack, "fsdp", 1)

    gate_now, up_now, down_now, _ = lax.optimization_barrier(
        (gate_weight, up_weight, down_weight, weight_pack)
    )
    piece_own, piece_near, piece_far = launch(
        deal_body(parts, count),
        [
            ((3, block, hidden_count), BF16),
            ((3, block, hidden_count), BF16),
            ((2, 3, block, hidden_count), BF16),
        ],
        [own_scalar],
        hbm([gate_now[0], up_now[0], down_now[0].T]),
        [pltpu.VMEM((parts, block, hidden_count), BF16)],
    )
    tables = (cosine, sine, early_pos, late_pos, row_pos)
    output_now, weight_far, weight_near, piece_far, tables = lax.optimization_barrier(
        (output_weight[0], weight_far, weight_near, piece_far, tables)
    )
    cosine, sine, early_pos, late_pos, row_pos = tables
    weights = [weight_pack, weight_near, weight_far, swap(weight_far, "fsdp", 1)]
    output_far = swap(output_now, "fsdp", 2)
    query, key_value = launch(
        project_body(parts, block),
        [((rows, QUERY_WIDTH), BF16), ((rows, 2 * KEY_WIDTH), BF16)],
        [own_scalar],
        [attend_input, cosine, sine, *hbm(weights)],
    )
    output_far, far_now = lax.optimization_barrier((output_far, piece_far, key_value))[:2]
    feed_far = swap(far_now, "fsdp", 2)
    key_values, extras = gather_levels(
        key_value,
        "ctx",
        [
            lambda token: (
                swap(after(output_now, token), "fsdp", 1),
                swap(after(piece_near, token), "fsdp", 1),
            ),
            lambda token: (swap(after(output_far, token), "fsdp", 1),),
        ],
    )
    output_blocks = [output_now, extras[0][0], output_far, extras[1][0]]
    feed_near = extras[0][1]
    feeds_far = swap(after(grad_feed, key_values[-2]), "fsdp", 2)

    mixed, log_total, middle, feed_input = launch(
        attend_body(parts, count, half),
        [
            ((rows, QUERY_WIDTH), BF16),
            ((KEY_HEADS, 2 * GROUP * half), F32),
            ((rows, width), F32),
            ((parts, rows, padded), BF16),
        ],
        [own_scalar],
        [
            query,
            early_pos,
            late_pos,
            row_pos,
            both_rows,
            feedforward_gain,
            *key_values,
            *hbm(output_blocks),
        ],
        [
            pltpu.VMEM((count * half, 2 * KEY_WIDTH), BF16),
            pltpu.VMEM((count * half, 2 * KEY_WIDTH), BF16),
            pltpu.VMEM((parts, rows, block), F32),
        ],
    )
    input_far = swap(feed_input, "fsdp", 2)
    near_now, far_now, feed_far = lax.optimization_barrier(
        (grad_feed, feeds_far, feed_far, input_far)
    )[:3]
    feeds = [grad_feed, swap(near_now, "fsdp", 1), feeds_far, swap(far_now, "fsdp", 1)]
    feed_weights = [piece_own, feed_near, feed_far, swap(feed_far[1], "fsdp", 1)]
    feed_inputs = [
        feed_input,
        swap(feed_input, "fsdp", 1),
        input_far,
        swap(input_far, "fsdp", 1),
    ]
    kept, sent, hidden_units, grad_gate, grad_up = launch(
        feed_body(parts, block),
        [((2, parts, rows, padded), BF16)] * 2 + [((parts * rows, hidden_count), BF16)] * 3,
        [own_scalar],
        [*feed_inputs, *feeds, *hbm(feed_weights)],
    )
    received = swap(sent, "fsdp", 1)
    passed = (kept[1].astype(F32) + received[1].astype(F32)).astype(BF16)
    passed, hidden_units, grad_gate, grad_up = lax.optimization_barrier(
        (passed, hidden_units, grad_gate, grad_up)
    )
    passed = swap(passed, "fsdp", 2)
    down_kept, down_sent, gate_kept, gate_sent, up_kept, up_sent = launch(
        feed_grads_body(parts, count, block),
        [((count // 2, parts * share, block), BF16, True)] * 6,
        [own_scalar, side_scalar],
        [*feed_inputs, *feeds, hidden_units, grad_gate, grad_up],
    )
    down_received = swap(down_sent, "ctx", 1)
    passed = after(passed, down_sent)
    input_far = swap(after(attend_input, passed), "fsdp", 2)

    grad_middle, pack, feed_gain_part, pair_kept, pair_sent = launch(
        back_body(parts, count, half, block),
        [((rows, width), F32), ((3, parts, rows, padded), BF16, True), ((1, width), F32)]
        + [((count // 2, rows, 2 * KEY_WIDTH), BF16)] * 2,
        [own_scalar],
        [
            kept,
            received,
            passed,
            middle,
            feedforward_gain,
            both_rows,
            mixed,
            query,
            log_total,
            early_pos,
            late_pos,
            row_pos,
            cosine,
            sine,
            *key_values,
            *hbm(output_blocks),
        ],
        [
            pltpu.VMEM((count * half, 2 * KEY_WIDTH), BF16),
            pltpu.VMEM((count * half, 2 * KEY_WIDTH), BF16),
        ],
    )

    bits = bits_of("ctx")
    pair_sent, input_near, input_far, hidden_units, down_received = lax.optimization_barrier(
        (pair_sent, attend_input, input_far, hidden_units, down_received)
    )
    pair_received = swap(pair_sent, "ctx", 1)

    def next_step(kept, received, k, *gates):
        received = after(received, *gates)
        total = (kept.astype(F32) + received.astype(F32)).astype(BF16)
        kept, sent = split_side(total, own_ctx, k + 1)
        return kept, sent, swap(sent, "ctx", bits[k + 1])

    def last_step(kept, received, k, *gates):
        received = after(received, *gates)
        for n in range(k, len(bits) - 1):
            kept, _, received = next_step(kept, received, n)
        return (kept.astype(F32) + received.astype(F32))[0]

    pack_far = swap(pack, "fsdp", 2)
    pack_near = swap(pack, "fsdp", 1)
    inputs_swapped = swap(input_near, "fsdp", 1), swap(input_far, "fsdp", 1)
    down_kept, down_sent, down_received = next_step(down_kept, down_received, 0)
    out_kept, out_sent = launch(
        feed_out_body(parts, rows),
        [((2, parts, rows, padded), BF16)] * 2,
        [own_scalar],
        [*down_weights(feed_weights), hidden_units],
    )
    pair_received, pack_far, pack_near, inputs_swapped, out_sent, _ = lax.optimization_barrier(
        (pair_received, pack_far, pack_near, inputs_swapped, out_sent, down_sent)
    )
    gate_received = swap(after(gate_sent, pair_received), "ctx", 1)
    pair_kept, pair_sent = half_step(pair_kept, pair_received)
    pair_received = swap(pair_sent, "ctx", bits[1])
    pack_far, down_received, out_sent, _ = lax.optimization_barrier(
        (pack_far, down_received, out_sent, pair_sent)
    )
    if len(bits) > 2:
        down_kept, down_sent, down_received = next_step(down_kept, down_received, 1)
    packs = [pack, pack_near, pack_far, swap(pack_far, "fsdp", 1)]
    input_all = [attend_input, inputs_swapped[0], input_far, inputs_swapped[1]]
    up_received = swap(after(up_sent, pair_received), "ctx", 1)
    rest_kept, rest_sent = launch(
        attention_grads_body(parts, count, block),
        [((count // 2, 2 * QUERY_WIDTH // count, block), BF16, True)] * 2,
        [own_scalar, side_scalar],
        [*hbm(packs), *hbm(input_all)],
    )
    pair_received, out_now, _ = lax.optimization_barrier((pair_received, out_sent, rest_sent))
    for bit in bits[2:]:
        pair_kept, pair_sent = half_step(pair_kept, pair_received)
        pair_received = swap(pair_sent, "ctx", bit)
    rest_received = swap(after(rest_sent, pair_sent), "ctx", 1)
    pair_received = after(pair_received, down_sent)
    out_received = swap(after(out_now, pair_sent), "fsdp", 1)
    pair_in, input_grad, attention_gain_part = launch(
        input_grad_body(parts, block),
        [((rows, 2 * KEY_WIDTH), BF16), ((width, rows), F32), ((1, width), F32)],
        [own_scalar],
        [
            pair_kept,
            pair_received,
            cosine,
            sine,
            pack,
            both_rows,
            attention_gain,
            grad_middle,
            *hbm(weights),
        ],
        [pltpu.VMEM((parts, rows, block), F32)],
    )
    pair_far = swap(pair_in, "fsdp", 2)
    pair_near = swap(pair_in, "fsdp", 1)
    gains = jnp.concatenate([attention_gain_part, feed_gain_part], axis=0)
    gains = gains + swap(gains, "fsdp", 2)
    gate_kept, gate_part, gate_received = next_step(gate_kept, gate_received, 0, pair_in)
    out_received = after(out_received, pair_in)
    out_passed = (out_kept[1].astype(F32) + out_received[1].astype(F32)).astype(BF16)
    pair_far, gains, _ = lax.optimization_barrier((pair_far, gains, gate_part))
    pair_all = [pair_in, pair_near, pair_far, swap(pair_far, "fsdp", 1)]
    gains = gains + swap(gains, "fsdp", 1)
    up_kept, up_part, up_received = next_step(up_kept, up_received, 0, pair_far)
    pair_all[3], gains, _ = lax.optimization_barrier((pair_all[3], gains, up_part))
    pair_grad_kept, pair_grad_sent = launch(
        pair_grads_body(parts, count, block),
        [((count // 2, 2 * KEY_WIDTH // count, block), BF16)] * 2,
        [own_scalar, side_scalar],
        [*pair_all, *hbm(input_all)],
    )
    gains = after(gains, pair_grad_sent)
    pair_grad_received = swap(pair_grad_sent, "ctx", 1)
    gains = gains + swap(gains, "ctx", 1)
    out_passed = swap(after(out_passed, pair_grad_sent), "fsdp", 2)
    gate_part = up_part = pair_grad_sent
    for k in range(1, len(bits) - 1):
        gate_kept, gate_part, gate_received = next_step(gate_kept, gate_received, k, gate_part)
        up_kept, up_part, up_received = next_step(up_kept, up_received, k, gate_part)
    down_own = last_step(down_kept, down_received, min(2, len(bits) - 1), pair_grad_sent)
    for k in range(len(bits) - 1):
        rest_kept, rest_part, rest_received = next_step(
            rest_kept, rest_received, k, pair_grad_sent
        )
        pair_grad_kept, pair_grad_sent, pair_grad_received = next_step(
            pair_grad_kept, pair_grad_received, k, rest_part
        )
        gains = after(gains, pair_grad_sent)
        gains = gains + swap(gains, "ctx", bits[k + 1])
    middle = after(middle, up_part)
    gate_own = (gate_kept.astype(F32) + gate_received.astype(F32))[0]
    up_own = (up_kept.astype(F32) + up_received.astype(F32))[0]
    rest_own = (rest_kept.astype(F32) + rest_received.astype(F32))[0]
    pair_own = (pair_grad_kept.astype(F32) + pair_grad_received.astype(F32))[0]
    (block_output,) = launch(
        output_body(parts, block),
        [((width, rows), F32)],
        [],
        [middle, out_kept, out_received, out_passed],
    )
    query_rows, key_rows = QUERY_WIDTH // count, KEY_WIDTH // count
    query_own, output_own = rest_own[:query_rows], rest_own[query_rows:]

    stacked = jnp.concatenate([down_own, gate_own, up_own], axis=0).astype(BF16)
    stacked = stacked.reshape(3, parts, share, block).transpose(1, 0, 2, 3)
    arrived = jnp.stack(exchange_blocks([stacked[j] for j in range(parts)], "fsdp"))
    ordered = jnp.concatenate(
        [lax.dynamic_index_in_dim(arrived, own ^ b, 0, keepdims=False) for b in range(parts)],
        axis=1,
    ).astype(F32)

    return (
        block_output.T[None],
        input_grad.T[None],
        query_own.T[None],
        pair_own[:key_rows].T[None],
        pair_own[key_rows:].T[None],
        output_own[None],
        ordered[1].T[None],
        ordered[2].T[None],
        ordered[0][None],
        gains[:1],
        gains[1:],
    )


def solution(mesh):
    return jax.shard_map(
        shards,
        mesh=mesh,
        in_specs=(
            P("fsdp", "ctx", None),
            P(),
            P(None, "fsdp", None),
            P(None, "fsdp", None),
            P(None, "fsdp", None),
            P(None, None, "fsdp"),
            P(None, "fsdp", None),
            P(None, "fsdp", None),
            P(None, None, "fsdp"),
            P(),
            P(),
            P("fsdp", "ctx", None),
        ),
        out_specs=(
            P("fsdp", "ctx", None),
            P("fsdp", "ctx", None),
            P(None, "fsdp", "ctx"),
            P(None, "fsdp", "ctx"),
            P(None, "fsdp", "ctx"),
            P(None, "ctx", "fsdp"),
            P(None, "fsdp", "ctx"),
            P(None, "fsdp", "ctx"),
            P(None, "ctx", "fsdp"),
            P(),
            P(),
        ),
        check_vma=False,
    )
```

profile of v0, /device:TPU:0, one launch (start us, length us, event | category | flops | bytes accessed | tf_op | source)
XLA Modules:
  0.0 257.6 jit_solution(13272686273827079829)
XLA Ops:
  0.7 4.3 %shard_map.203 = (bf16[240,1600]{1,0:T(8,128)(2,1)}, bf16[4,128,256]{2,1,0:T(8,128)(2,1)}, bf16[4,128,256]{2,1,0:T(8,128)(2,1)}, f32[2,128,960]{2,1,0:T(8,128)}) custom-call(f32[960,128]{1,0:T(8,128)} %bitcast.166, f32[960,128]{1,0:T(8,128)} %bitcast.167, f32[1,960]{1,0:T(1,128)} %refs_7_.1, bf16[240,960]{1,0:T(8,128)(2,1)} %bitcast.168, ...), custom_call_target="tpu_custom_call" | custom-call | tf_op jit(solution)/shard_map/pallas_call | solution.py:190
  9.1 5.6 %shard_map.204 = (bf16[3,240,640]{2,1,0:T(8,128)(2,1)}, bf16[3,240,640]{2,1,0:T(8,128)(2,1)}, bf16[2,3,240,640]{3,2,1,0:T(8,128)(2,1)}) custom-call(s32[1]{0:T(128)} %bitcast.refs_0_, bf16[240,2560]{1,0:T(8,128)(2,1)} %bitcast.161, bf16[240,2560]{1,0:T(8,128)(2,1)} %bitcast.162, bf16[240,2560]{1,0:T(8,128)(2,1)} %bitcast.163), custom_call_target="tpu_custom_call" | custom-call | tf_op jit(solution)/shard_map/pallas_call | solution.py:190
  16.6 9.4 %collective-permute-done.refs_6_.refs_11_ = bf16[240,1600]{1,0:T(8,128)(2,1)S(1)} collective-permute-done((bf16[240,1600]{1,0:T(8,128)(2,1)}, bf16[240,1600]{1,0:T(8,128)(2,1)S(1)}, u32[]{:S(2)}, u32[]{:S(2)}) %collective-permute-start) | collective-permute-done | bytes 768032 | tf_op jit(solution)/shard_map/ppermute | solution.py:37
  29.2 4.4 %shard_map.205 = (bf16[128,960]{1,0:T(8,128)(2,1)}, bf16[128,640]{1,0:T(8,128)(2,1)}) custom-call(s32[1]{0:T(128)} %bitcast.refs_0_, bf16[4,128,256]{2,1,0:T(8,128)(2,1)} %get-tuple-element.186.refs_1_.refs_6_, f32[128,128]{1,0:T(8,128)} %pad_maximum_fusion.2.refs_2_.refs_13_.refs_3_, f32[128,128]{1,0:T(8,128)} %pad_maximum_fusion.3.refs_3_.refs_14_.refs_4_, ...), custom_call_target="tpu_custom_call" | custom-call | tf_op jit(solution)/shard_map/pallas_call | solution.py:190
  33.6 6.1 %collective-permute-done.11.refs_17_.refs_25_ = bf16[960,240]{1,0:T(8,128)(2,1)S(1)} collective-permute-done((bf16[960,240]{1,0:T(8,128)(2,1)S(1)}, bf16[960,240]{1,0:T(8,128)(2,1)S(1)}, u32[]{:S(2)}, u32[]{:S(2)}) %collective-permute-start.11) | collective-permute-done | bytes 460832 | tf_op jit(solution)/shard_map/ppermute | solution.py:37
  50.8 7.3 %collective-permute-done.5.refs_11_.refs_19_ = bf16[128,640]{1,0:T(8,128)(2,1)S(1)} collective-permute-done((bf16[128,640]{1,0:T(8,128)(2,1)}, bf16[128,640]{1,0:T(8,128)(2,1)S(1)}, u32[]{:S(2)}, u32[]{:S(2)}) %collective-permute-start.5) | collective-permute-done | bytes 163872 | tf_op jit(solution)/shard_map/ppermute | solution.py:37
  61.1 3.9 %collective-permute-done.10.refs_13_.refs_21_ = bf16[128,640]{1,0:T(8,128)(2,1)} collective-permute-done((bf16[128,640]{1,0:T(8,128)(2,1)S(1)}, bf16[128,640]{1,0:T(8,128)(2,1)}, u32[]{:S(2)}, u32[]{:S(2)}) %collective-permute-start.10) | collective-permute-done | bytes 163872 | tf_op jit(solution)/shard_map/ppermute | solution.py:37
  75.3 8.6 %shard_map.206 = (bf16[128,960]{1,0:T(8,128)(2,1)}, f32[5,384]{1,0:T(8,128)}, f32[128,960]{1,0:T(8,128)}, bf16[4,128,256]{2,1,0:T(8,128)(2,1)}) custom-call(s32[1]{0:T(128)} %bitcast.refs_0_, bf16[128,960]{1,0:T(8,128)(2,1)} %get-tuple-element.135.refs_1_.refs_8_, s32[512,1]{1,0:T(8,128)} %copy.55.refs_2_.refs_10_, s32[512,1]{1,0:T(8,128)} %copy.56.refs_3_.refs_11_, ...), custom_call_target="tpu_custom_call" | custom-call | tf_op jit(solution)/shard_map/pallas_call | solution.py:190
  84.6 4.1 %collective-permute-done.17.refs_7_.refs_8_ = bf16[4,128,256]{2,1,0:T(8,128)(2,1)S(1)} collective-permute-done((bf16[4,128,256]{2,1,0:T(8,128)(2,1)S(1)}, bf16[4,128,256]{2,1,0:T(8,128)(2,1)S(1)}, u32[]{:S(2)}, u32[]{:S(2)}) %collective-permute-start.17) | collective-permute-done | bytes 262176 | tf_op jit(solution)/shard_map/ppermute | solution.py:37
  88.6 4.3 %collective-permute-done.15.refs_3_.refs_4_ = bf16[4,128,256]{2,1,0:T(8,128)(2,1)S(1)} collective-permute-done((bf16[4,128,256]{2,1,0:T(8,128)(2,1)}, bf16[4,128,256]{2,1,0:T(8,128)(2,1)S(1)}, u32[]{:S(2)}, u32[]{:S(2)}) %collective-permute-start.15) | collective-permute-done | bytes 262176 | tf_op jit(solution)/shard_map/ppermute | solution.py:37
  98.6 9.7 %shard_map.207 = (bf16[2,4,128,256]{3,2,1,0:T(8,128)(2,1)}, bf16[2,4,128,256]{3,2,1,0:T(8,128)(2,1)}, bf16[512,640]{1,0:T(8,128)(2,1)}, bf16[512,640]{1,0:T(8,128)(2,1)}, bf16[512,640]{1,0:T(8,128)(2,1)}) custom-call(s32[1]{0:T(128)} %bitcast.refs_0_, bf16[4,128,256]{2,1,0:T(8,128)(2,1)} %get-tuple-element.157.refs_1_.refs_2_, ...), custom_call_target="tpu_custom_call" | custom-call | tf_op jit(solution)/shard_map/pallas_call | solution.py:190
  111.7 5.5 %shard_map.208 = (bf16[4,320,240]{2,1,0:T(8,128)(2,1)}, bf16[4,320,240]{2,1,0:T(8,128)(2,1)}, bf16[4,320,240]{2,1,0:T(8,128)(2,1)}, bf16[4,320,240]{2,1,0:T(8,12...) custom-call(s32[1]{0:T(128)} %bitcast.refs_0_, s32[1]{0:T(128)} %bitcast.17.refs_1_, ...), custom_call_target="tpu_custom_call" | custom-call | tf_op jit(solution)/shard_map/pallas_call | solution.py:190
  120.6 6.6 %collective-permute-done.23.refs_3_ = bf16[4,128,256]{2,1,0:T(8,128)(2,1)S(1)} collective-permute-done((bf16[4,128,256]{2,1,0:T(8,128)(2,1)S(1)}, bf16[4,128,256]{2,1,0:T(8,128)(2,1)S(1)}, u32[]{:S(2)}, u32[]{:S(2)}) %collective-permute-start.23) | collective-permute-done | bytes 262176 | tf_op jit(solution)/shard_map/ppermute | solution.py:37
  128.7 12.1 %shard_map.209 = (f32[128,960]{1,0:T(8,128)}, bf16[3,4,128,256]{3,2,1,0:T(8,128)(2,1)}, f32[1,960]{1,0:T(1,128)}, bf16[4,128,640]{2,1,0:T(8,128)(2,1)}, bf16[4,128,640]{2,1,0:T(8,128)(2,1)}) custom-call(s32[1]{0:T(128)} %bitcast.refs_0_, bf16[2,4,128,256]{3,2,1,0:T(8,128)(2,1)} %get-tuple-element.166.refs_1_, bf16[2,4,128,256]{3,2,1,0:T(8,128)(2,1)} %copy-done.13, ...), custom_call_target="tpu_custom_call" | custom-call | tf_op jit(solution)/shard_map/pallas_call | solution.py:190
  142.6 5.5 %shard_map.210 = (bf16[2,4,128,256]{3,2,1,0:T(8,128)(2,1)}, bf16[2,4,128,256]{3,2,1,0:T(8,128)(2,1)}) custom-call(s32[1]{0:T(128)} %bitcast.refs_0_, bf16[3,240,640]{2,1,0:T(8,128)(2,1)} %get-tuple-element.163.refs_9_.refs_1_, bf16[3,240,640]{2,1,0:T(8,128)(2,1)} %copy-done.1, bf16[2,3,240,640]{3,2,1,0:T(8,128)(2,1)} %copy-done, ...), custom_call_target="tpu_custom_call" | custom-call | tf_op jit(solution)/shard_map/pallas_call | solution.py:190
  151.2 8.2 %collective-permute-done.27.refs_4_ = bf16[3,4,128,256]{3,2,1,0:T(8,128)(2,1)} collective-permute-done((bf16[3,4,128,256]{3,2,1,0:T(8,128)(2,1)}, bf16[3,4,128,256]{3,2,1,0:T(8,128)(2,1)}, u32[]{:S(2)}, u32[]{:S(2)}) %collective-permute-start.27) | collective-permute-done | bytes 786464 | tf_op jit(solution)/shard_map/ppermute | solution.py:37
  164.9 4.0 %shard_map.211 = (bf16[4,240,240]{2,1,0:T(8,128)(2,1)}, bf16[4,240,240]{2,1,0:T(8,128)(2,1)}) custom-call(s32[1]{0:T(128)} %bitcast.refs_0_, s32[1]{0:T(128)} %bitcast.17.refs_1_, bf16[3,4,128,256]{3,2,1,0:T(8,128)(2,1)} %get-tuple-element.185.refs_2_.refs_5_, bf16[3,4,128,256]{3,2,1,0:T(8,128)(2,1)} %collective-permute-done.28.refs_3_, ...), custom_call_target="tpu_custom_call" | custom-call | tf_op jit(solution)/shard_map/pallas_call | solution.py:190
  179.4 9.1 %collective-permute-done.35.refs_2_ = bf16[1,128,640]{2,1,0:T(8,128)(2,1)S(1)} collective-permute-done((bf16[1,128,640]{2,1,0:T(8,128)(2,1)S(1)}, bf16[1,128,640]{2,1,0:T(8,128)(2,1)S(1)}, u32[]{:S(2)}, u32[]{:S(2)}) %collective-permute-start.35) | collective-permute-done | bytes 163872 | tf_op jit(solution)/shard_map/ppermute | solution.py:37
  189.2 6.7 %shard_map.212 = (bf16[128,640]{1,0:T(8,128)(2,1)}, f32[960,128]{1,0:T(8,128)}, f32[1,960]{1,0:T(1,128)}) custom-call(s32[1]{0:T(128)} %bitcast.refs_0_, bf16[1,128,640]{2,1,0:T(8,128)(2,1)} %get-tuple-element.286.refs_1_, bf16[1,128,640]{2,1,0:T(8,128)(2,1)} %copy-done.38, f32[128,128]{1,0:T(8,128)} %pad_maximum_fusion.2.refs_2_.refs_13_.refs_3_, ...), custom_call_target="tpu_custom_call" | custom-call | tf_op jit(solution)/shard_map/pallas_call | solution.py:190
  206.4 3.5 %shard_map.213 = (bf16[4,80,240]{2,1,0:T(8,128)(2,1)}, bf16[4,80,240]{2,1,0:T(8,128)(2,1)}) custom-call(s32[1]{0:T(128)} %bitcast.refs_0_, s32[1]{0:T(128)} %bitcast.17.refs_1_, bf16[128,640]{1,0:T(8,128)(2,1)} %get-tuple-element.206.refs_2_, bf16[128,640]{1,0:T(8,128)(2,1)} %copy-done.41, bf16[128,640]{1,0:T(8,128)(2,1)} %copy-done.40, ...), custom_call_target="tpu_custom_call" | custom-call | tf_op jit(solution)/shard_map/pallas_call | solution.py:190
  217.9 3.4 %collective-permute-start.53 = (bf16[1,320,240]{2,1,0:T(8,128)(2,1)}, bf16[1,320,240]{2,1,0:T(8,128)(2,1)S(1)}, u32[]{:S(2)}, u32[]{:S(2)}) collective-permute-start(bf16[1,320,240]{2,1,0:T(8,128)(2,1)} %constant_dynamic-slice_fusion.5), channel_id=1, source_target_pairs={{0,16},{4,20},{8,24},{12,28},{16,0},{20,4},{24,8},{28,12},{1,17},{... | collective-permute-start | bytes 460808 | tf_op jit(solution)/shard_map/ppermute | solution.py:37
  226.3 3.8 %collective-permute-start.54 = (bf16[1,320,240]{2,1,0:T(8,128)(2,1)S(1)}, bf16[1,320,240]{2,1,0:T(8,128)(2,1)S(1)}, u32[]{:S(2)}, u32[]{:S(2)}) collective-permute-start(bf16[1,320,240]{2,1,0:T(8,128)(2,1)S(1)} %constant_dynamic-slice_fusion.4), channel_id=1, source_target_pairs={{0,16},{4,20},{8,24},{12,28},{16,0},{20,4},{24,8},{28,12},{1,17},{... | collective-permute-start | bytes 460808 | tf_op jit(solution)/shard_map/ppermute | solution.py:37
  232.4 4.4 %collective-permute-done.50 = bf16[2,80,240]{2,1,0:T(8,128)(2,1)S(1)} collective-permute-done((bf16[2,80,240]{2,1,0:T(8,128)(2,1)S(1)}, bf16[2,80,240]{2,1,0:T(8,128)(2,1)S(1)}, u32[]{:S(2)}, u32[]{:S(2)}) %collective-permute-start.50) | collective-permute-done | bytes 76832 | tf_op jit(solution)/shard_map/ppermute | solution.py:37
  240.1 3.2 %collective-permute-done.60 = f32[2,960]{1,0:T(2,128)S(1)} collective-permute-done((f32[2,960]{1,0:T(2,128)S(1)}, f32[2,960]{1,0:T(2,128)S(1)}, u32[]{:S(2)}, u32[]{:S(2)}) %collective-permute-start.60) | collective-permute-done | bytes 7712 | tf_op jit(solution)/shard_map/ppermute | solution.py:37
  (269 shorter events, 112.7 us)
Async XLA Ops:
  4.9 21.0 %collective-permute-start = (bf16[240,1600]{1,0:T(8,128)(2,1)}, bf16[240,1600]{1,0:T(8,128)(2,1)S(1)}, u32[]{:S(2)}, u32[]{:S(2)}) collective-permute-start(bf16[240,1600]{1,0:T(8,128)(2,1)} %get-tuple-element.126.refs_4_.refs_9_), channel_id=1, source_target_pairs={{0,2},{1,3},{2,0},{3,1},{4,6},{5,7},{6,4},{7,5},{8,10},{9,11},{10,... | collective-permute-start | bytes 2304008 | tf_op jit(solution)/shard_map/ppermute | solution.py:37
  7.9 18.0 %collective-permute-start.1 = (bf16[240,1600]{1,0:T(8,128)(2,1)}, bf16[240,1600]{1,0:T(8,128)(2,1)S(1)}, u32[]{:S(2)}, u32[]{:S(2)}) collective-permute-start(bf16[240,1600]{1,0:T(8,128)(2,1)} %get-tuple-element.126.refs_4_.refs_9_), channel_id=1, source_target_pairs={{0,1},{1,0},{2,3},{3,2},{4,5},{5,4},{6,7},{7,6},{8,9},{9,8},{10,11... | collective-permute-start | bytes 2304008 | tf_op jit(solution)/shard_map/ppermute | solution.py:37
  26.0 13.6 %collective-permute-start.11 = (bf16[960,240]{1,0:T(8,128)(2,1)S(1)}, bf16[960,240]{1,0:T(8,128)(2,1)S(1)}, u32[]{:S(2)}, u32[]{:S(2)}) collective-permute-start(bf16[960,240]{1,0:T(8,128)(2,1)S(1)} %bitcast.159), channel_id=1, source_target_pairs={{0,2},{1,3},{2,0},{3,1},{4,6},{5,7},{6,4},{7,5},{8,10},{9,11},{10,... | collective-permute-start | bytes 1382408 | tf_op jit(solution)/shard_map/ppermute | solution.py:37
  39.7 53.2 %collective-permute-start.18 = (bf16[2,3,240,640]{3,2,1,0:T(8,128)(2,1)}, bf16[2,3,240,640]{3,2,1,0:T(8,128)(2,1)S(1)}, u32[]{:S(2)}, u32[]{:S(2)}) collective-permute-start(bf16[2,3,240,640]{3,2,1,0:T(8,128)(2,1)} %get-tuple-element.160), channel_id=1, source_target_pairs={{0,2},{1,3},{2,0},{3,1},{4,6},{5,7},{6,4},{7,5},{8,10},{9,11},{10,... | collective-permute-start | bytes 5529608 | tf_op jit(solution)/shard_map/ppermute | solution.py:37
  41.4 16.7 %collective-permute-start.7 = (bf16[3,240,640]{2,1,0:T(8,128)(2,1)}, bf16[3,240,640]{2,1,0:T(8,128)(2,1)S(1)}, u32[]{:S(2)}, u32[]{:S(2)}) collective-permute-start(bf16[3,240,640]{2,1,0:T(8,128)(2,1)} %get-tuple-element.144), channel_id=1, source_target_pairs={{0,1},{1,0},{2,3},{3,2},{4,5},{5,4},{6,7},{7,6},{8,9},{9,8},{10,11... | collective-permute-start | bytes 2764808 | tf_op jit(solution)/shard_map/ppermute | solution.py:37
  41.4 16.7 %collective-permute-start.6 = (bf16[960,240]{1,0:T(8,128)(2,1)S(1)}, bf16[960,240]{1,0:T(8,128)(2,1)S(1)}, u32[]{:S(2)}, u32[]{:S(2)}) collective-permute-start(bf16[960,240]{1,0:T(8,128)(2,1)S(1)} %bitcast.160), channel_id=1, source_target_pairs={{0,1},{1,0},{2,3},{3,2},{4,5},{5,4},{6,7},{7,6},{8,9},{9,8},{10,11... | collective-permute-start | bytes 1382408 | tf_op jit(solution)/shard_map/ppermute | solution.py:37
  72.7 15.9 %collective-permute-start.17 = (bf16[4,128,256]{2,1,0:T(8,128)(2,1)S(1)}, bf16[4,128,256]{2,1,0:T(8,128)(2,1)S(1)}, u32[]{:S(2)}, u32[]{:S(2)}) collective-permute-start(bf16[4,128,256]{2,1,0:T(8,128)(2,1)S(1)} %copy-done.14), channel_id=1, source_target_pairs={{0,2},{1,3},{2,0},{3,1},{4,6},{5,7},{6,4},{7,5},{8,10},{9,11},{10,... | collective-permute-start | bytes 786440 | tf_op jit(solution)/shard_map/ppermute | solution.py:37
  117.3 24.3 %collective-permute-start.25 = (bf16[4,320,240]{2,1,0:T(8,128)(2,1)}, bf16[4,320,240]{2,1,0:T(8,128)(2,1)}, u32[]{:S(2)}, u32[]{:S(2)}) collective-permute-start(bf16[4,320,240]{2,1,0:T(8,128)(2,1)} %get-tuple-element.177), channel_id=1, source_target_pairs={{0,4},{4,0},{8,12},{12,8},{16,20},{20,16},{24,28},{28,24},{1,5},{5... | collective-permute-start | bytes 1843208 | tf_op jit(solution)/shard_map/ppermute | solution.py:37
  127.2 14.4 %collective-permute-start.24 = (bf16[4,128,256]{2,1,0:T(8,128)(2,1)S(1)}, bf16[4,128,256]{2,1,0:T(8,128)(2,1)S(1)}, u32[]{:S(2)}, u32[]{:S(2)}) collective-permute-start(bf16[4,128,256]{2,1,0:T(8,128)(2,1)S(1)} %copy-done.6), channel_id=1, source_target_pairs={{0,2},{1,3},{2,0},{3,1},{4,6},{5,7},{6,4},{7,5},{8,10},{9,11},{10,... | collective-permute-start | bytes 786440 | tf_op jit(solution)/shard_map/ppermute | solution.py:37
  140.8 18.6 %collective-permute-start.27 = (bf16[3,4,128,256]{3,2,1,0:T(8,128)(2,1)}, bf16[3,4,128,256]{3,2,1,0:T(8,128)(2,1)}, u32[]{:S(2)}, u32[]{:S(2)}) collective-permute-start(bf16[3,4,128,256]{3,2,1,0:T(8,128)(2,1)} %get-tuple-element.185.refs_2_.refs_5_), channel_id=1, source_target_pairs={{0,2},{1,3},{2,0},{3,1},{4,6},{5,7},{6,4},{7,5},{8,10},{9,11},{10,... | collective-permute-start | bytes 2359304 | tf_op jit(solution)/shard_map/ppermute | solution.py:37
  141.5 17.9 %collective-permute-start.28 = (bf16[3,4,128,256]{3,2,1,0:T(8,128)(2,1)}, bf16[3,4,128,256]{3,2,1,0:T(8,128)(2,1)}, u32[]{:S(2)}, u32[]{:S(2)}) collective-permute-start(bf16[3,4,128,256]{3,2,1,0:T(8,128)(2,1)} %get-tuple-element.185.refs_2_.refs_5_), channel_id=1, source_target_pairs={{0,1},{1,0},{2,3},{3,2},{4,5},{5,4},{6,7},{7,6},{8,9},{9,8},{10,11... | collective-permute-start | bytes 2359304 | tf_op jit(solution)/shard_map/ppermute | solution.py:37
  141.6 17.9 %collective-permute-start.26 = (bf16[4,128,640]{2,1,0:T(8,128)(2,1)}, bf16[4,128,640]{2,1,0:T(8,128)(2,1)}, u32[]{:S(2)}, u32[]{:S(2)}) collective-permute-start(bf16[4,128,640]{2,1,0:T(8,128)(2,1)} %get-tuple-element.184), channel_id=1, source_target_pairs={{0,4},{4,0},{8,12},{12,8},{16,20},{20,16},{24,28},{28,24},{1,5},{5... | collective-permute-start | bytes 1966088 | tf_op jit(solution)/shard_map/ppermute | solution.py:37
  163.2 33.8 %collective-permute-start.38 = (bf16[4,320,240]{2,1,0:T(8,128)(2,1)}, bf16[4,320,240]{2,1,0:T(8,128)(2,1)S(1)}, u32[]{:S(2)}, u32[]{:S(2)}) collective-permute-start(bf16[4,320,240]{2,1,0:T(8,128)(2,1)} %get-tuple-element.211), channel_id=1, source_target_pairs={{0,4},{4,0},{8,12},{12,8},{16,20},{20,16},{24,28},{28,24},{1,5},{5... | collective-permute-start | bytes 1843208 | tf_op jit(solution)/shard_map/ppermute | solution.py:37
  173.7 14.8 %collective-permute-start.35 = (bf16[1,128,640]{2,1,0:T(8,128)(2,1)S(1)}, bf16[1,128,640]{2,1,0:T(8,128)(2,1)S(1)}, u32[]{:S(2)}, u32[]{:S(2)}) collective-permute-start(bf16[1,128,640]{2,1,0:T(8,128)(2,1)S(1)} %get-tuple-element.285), channel_id=1, source_target_pairs={{0,16},{4,20},{8,24},{12,28},{16,0},{20,4},{24,8},{28,12},{1,17},{... | collective-permute-start | bytes 491528 | tf_op jit(solution)/shard_map/ppermute | solution.py:37
  177.1 34.5 %collective-permute-start.52 = (bf16[1,320,240]{2,1,0:T(8,128)(2,1)}, bf16[1,320,240]{2,1,0:T(8,128)(2,1)}, u32[]{:S(2)}, u32[]{:S(2)}) collective-permute-start(bf16[1,320,240]{2,1,0:T(8,128)(2,1)} %constant_dynamic-slice_fusion.6), channel_id=1, source_target_pairs={{0,16},{4,20},{8,24},{12,28},{16,0},{20,4},{24,8},{28,12},{1,17},{... | collective-permute-start | bytes 460808 | tf_op jit(solution)/shard_map/ppermute | solution.py:37
  177.4 24.8 %collective-permute-start.32 = (bf16[4,320,240]{2,1,0:T(8,128)(2,1)}, bf16[4,320,240]{2,1,0:T(8,128)(2,1)S(1)}, u32[]{:S(2)}, u32[]{:S(2)}) collective-permute-start(bf16[4,320,240]{2,1,0:T(8,128)(2,1)} %get-tuple-element.193), channel_id=1, source_target_pairs={{0,4},{4,0},{8,12},{12,8},{16,20},{20,16},{24,28},{28,24},{1,5},{5... | collective-permute-start | bytes 1843208 | tf_op jit(solution)/shard_map/ppermute | solution.py:37
  177.9 32.0 %collective-permute-start.46 = (bf16[4,240,240]{2,1,0:T(8,128)(2,1)}, bf16[4,240,240]{2,1,0:T(8,128)(2,1)S(1)}, u32[]{:S(2)}, u32[]{:S(2)}) collective-permute-start(bf16[4,240,240]{2,1,0:T(8,128)(2,1)} %get-tuple-element.228), channel_id=1, source_target_pairs={{0,4},{4,0},{8,12},{12,8},{16,20},{20,16},{24,28},{28,24},{1,5},{5... | collective-permute-start | bytes 1382408 | tf_op jit(solution)/shard_map/ppermute | solution.py:37
  203.2 18.1 %collective-permute-start.44 = (bf16[2,4,128,256]{3,2,1,0:T(8,128)(2,1)}, bf16[2,4,128,256]{3,2,1,0:T(8,128)(2,1)S(1)}, u32[]{:S(2)}, u32[]{:S(2)}) collective-permute-start(bf16[2,4,128,256]{3,2,1,0:T(8,128)(2,1)} %get-tuple-element.223), channel_id=1, source_target_pairs={{0,1},{1,0},{2,3},{3,2},{4,5},{5,4},{6,7},{7,6},{8,9},{9,8},{10,11... | collective-permute-start | bytes 1572872 | tf_op jit(solution)/shard_map/ppermute | solution.py:37
  205.0 20.1 %collective-permute-start.39 = (bf16[2,320,240]{2,1,0:T(8,128)(2,1)}, bf16[2,320,240]{2,1,0:T(8,128)(2,1)S(1)}, u32[]{:S(2)}, u32[]{:S(2)}) collective-permute-start(bf16[2,320,240]{2,1,0:T(8,128)(2,1)} %dynamic-slice_bitcast_fusion), channel_id=1, source_target_pairs={{0,8},{4,12},{8,0},{12,4},{16,24},{20,28},{24,16},{28,20},{1,9},{5... | collective-permute-start | bytes 921608 | tf_op jit(solution)/shard_map/ppermute | solution.py:37
  209.9 15.2 %collective-permute-start.48 = (bf16[4,80,240]{2,1,0:T(8,128)(2,1)}, bf16[4,80,240]{2,1,0:T(8,128)(2,1)}, u32[]{:S(2)}, u32[]{:S(2)}) collective-permute-start(bf16[4,80,240]{2,1,0:T(8,128)(2,1)} %get-tuple-element.217), channel_id=1, source_target_pairs={{0,4},{4,0},{8,12},{12,8},{16,20},{20,16},{24,28},{28,24},{1,5},{5... | collective-permute-start | bytes 460808 | tf_op jit(solution)/shard_map/ppermute | solution.py:37
  214.6 16.8 %collective-permute-start.47 = (bf16[2,240,240]{1,2,0:T(8,128)(2,1)}, bf16[2,240,240]{1,2,0:T(8,128)(2,1)}, u32[]{:S(2)}, u32[]{:S(2)}) collective-permute-start(bf16[2,240,240]{1,2,0:T(8,128)(2,1)} %bitcast.170), channel_id=1, source_target_pairs={{0,8},{4,12},{8,0},{12,4},{16,24},{20,28},{24,16},{28,20},{1,9},{5... | collective-permute-start | bytes 691208 | tf_op jit(solution)/shard_map/ppermute | solution.py:37
  217.9 19.2 %collective-permute-start.53 = (bf16[1,320,240]{2,1,0:T(8,128)(2,1)}, bf16[1,320,240]{2,1,0:T(8,128)(2,1)S(1)}, u32[]{:S(2)}, u32[]{:S(2)}) collective-permute-start(bf16[1,320,240]{2,1,0:T(8,128)(2,1)} %constant_dynamic-slice_fusion.5), channel_id=1, source_target_pairs={{0,16},{4,20},{8,24},{12,28},{16,0},{20,4},{24,8},{28,12},{1,17},{... | collective-permute-start | bytes 460808 | tf_op jit(solution)/shard_map/ppermute | solution.py:37
  221.4 23.5 %collective-permute-start.45 = (bf16[4,128,256]{2,1,0:T(8,128)(2,1)S(1)}, bf16[4,128,256]{2,1,0:T(8,128)(2,1)S(1)}, u32[]{:S(2)}, u32[]{:S(2)}) collective-permute-start(bf16[4,128,256]{2,1,0:T(8,128)(2,1)S(1)} %fusion.7), channel_id=1, source_target_pairs={{0,2},{1,3},{2,0},{3,1},{4,6},{5,7},{6,4},{7,5},{8,10},{9,11},{10,... | collective-permute-start | bytes 786440 | tf_op jit(solution)/shard_map/ppermute | solution.py:37
  226.3 21.8 %collective-permute-start.54 = (bf16[1,320,240]{2,1,0:T(8,128)(2,1)S(1)}, bf16[1,320,240]{2,1,0:T(8,128)(2,1)S(1)}, u32[]{:S(2)}, u32[]{:S(2)}) collective-permute-start(bf16[1,320,240]{2,1,0:T(8,128)(2,1)S(1)} %constant_dynamic-slice_fusion.4), channel_id=1, source_target_pairs={{0,16},{4,20},{8,24},{12,28},{16,0},{20,4},{24,8},{28,12},{1,17},{... | collective-permute-start | bytes 460808 | tf_op jit(solution)/shard_map/ppermute | solution.py:37
  (83 other events, 568.0 us)
where the time goes:
time: 258 us
  waiting for transfers between devices  96.5 us (37%)
  Pallas kernels  72.3 us (28%)
  starting transfers between devices  56.4 us (22%)
  local copies, waits for them, and re-layouts  18.1 us (7%)
  other arithmetic  12.9 us (5%)
    ppermute x61, waiting for transfers between devices, swap(): return lax.ppermute(value, axis, [(i, i ^ bit) for i in range(size)])  96.5 us
    pallas_call x12, Pallas kernels, launch(): pl.pallas_call(wrapped, out_shape=[jax.ShapeDtypeStruct(o[0], o[1]) for o...  72.3 us
    ppermute x61, starting transfers between devices, swap(): return lax.ppermute(value, axis, [(i, i ^ bit) for i in range(size)])  56.4 us
    unnamed x94, local copies, waits for them, and re-layouts  7.22 us
  transfers between devices with their start and end apart: 61, of which 30 were waited for; matrix products, arithmetic and copies ran while one was open for 9% of the time, Pallas kernels for 20%

commit v1 on v0

--- a/solution.py
+++ b/solution.py
@@ -428,19 +428,18 @@
         sent_ref[c // 2, at : at + share] = jnp.where(first, odd, even).astype(BF16)
 
 
-def feed_grads_body(parts, count, block):
+def feed_grads_body(parts, count, block, left_count):
     def body(*refs):
         own = refs[0][0]
         first = refs[1][0] == 0
-        input_refs = refs[2 : 2 + parts]
-        feed_refs = refs[2 + parts : 2 + 2 * parts]
-        left_refs = refs[2 + 2 * parts : 5 + 2 * parts]
-        grad_refs = refs[5 + 2 * parts :]
+        right_refs = refs[2 : 2 + parts]
+        left_refs = refs[2 + parts : 2 + parts + left_count]
+        grad_refs = refs[2 + parts + left_count :]
         share = left_refs[0].shape[1] // count
-        for m in range(3):
+        for m in range(left_count):
             kept_ref, sent_ref = grad_refs[2 * m : 2 * m + 2]
             for j in range(parts):
-                rows_in = row_blocks(input_refs if m else feed_refs, block, own ^ j)
+                rows_in = row_blocks(right_refs, block, own ^ j)
                 grads = dot_tn(left_refs[m][...], rows_in)
                 put_units(kept_ref, sent_ref, first, j * share, grads, count)
             sent_ref.flush()
@@ -834,14 +833,21 @@
         (passed, hidden_units, grad_gate, grad_up)
     )
     passed = swap(passed, "fsdp", 2)
-    down_kept, down_sent, gate_kept, gate_sent, up_kept, up_sent = launch(
-        feed_grads_body(parts, count, block),
-        [((count // 2, parts * share, block), BF16, True)] * 6,
+    grads_shape = ((count // 2, parts * share, block), BF16, True)
+    down_kept, down_sent = launch(
+        feed_grads_body(parts, count, block, 1),
+        [grads_shape] * 2,
         [own_scalar, side_scalar],
-        [*feed_inputs, *feeds, hidden_units, grad_gate, grad_up],
+        [*feeds, hidden_units],
     )
     down_received = swap(down_sent, "ctx", 1)
-    passed = after(passed, down_sent)
+    gate_kept, gate_sent, up_kept, up_sent = launch(
+        feed_grads_body(parts, count, block, 2),
+        [grads_shape] * 4,
+        [own_scalar, side_scalar],
+        [*feed_inputs, after(grad_gate, down_sent), grad_up],
+    )
+    passed = after(passed, gate_sent)
     input_far = swap(after(attend_input, passed), "fsdp", 2)
 
     grad_middle, pack, feed_gain_part, pair_kept, pair_sent = launch(
@@ -965,7 +971,7 @@
     )
     gains = after(gains, pair_grad_sent)
     pair_grad_received = swap(pair_grad_sent, "ctx", 1)
-    gains = gains + swap(gains, "ctx", 1)
+    gains_received = swap(gains, "ctx", 1)
     out_passed = swap(after(out_passed, pair_grad_sent), "fsdp", 2)
     gate_part = up_part = pair_grad_sent
     for k in range(1, len(bits) - 1):
@@ -979,8 +985,12 @@
         pair_grad_kept, pair_grad_sent, pair_grad_received = next_step(
             pair_grad_kept, pair_grad_received, k, rest_part
         )
-        gains = after(gains, pair_grad_sent)
-        gains = gains + swap(gains, "ctx", bits[k + 1])
+        gains = gains + after(gains_received, pair_grad_sent)
+        gains_received = swap(gains, "ctx", bits[k + 1])
+        pair_grad_received, gains_received, rest_received = lax.optimization_barrier(
+            (pair_grad_received, gains_received, rest_received)
+        )
+    gains = gains + gains_received
     middle = after(middle, up_part)
     gate_own = (gate_kept.astype(F32) + gate_received.astype(F32))[0]
     up_own = (up_kept.astype(F32) + up_received.astype(F32))[0]

time: 258 us -> 250 us (0.969)
  waiting for transfers between devices: 96.5 us -> 78.4 us
  starting transfers between devices: 56.4 us -> 66.2 us
    ppermute x61, waiting for transfers between devices: 96.5 us -> 78.4 us  [swap(): return lax.ppermute(value, axis, [(i, i ^ bit) for i in range(size)])]
    ppermute x61, starting transfers between devices: 56.4 us -> 66.2 us  [swap(): return lax.ppermute(value, axis, [(i, i ^ bit) for i in range(size)])]
    pallas_call x12 -> x13, Pallas kernels: 72.3 us -> 74.6 us  [launch(): pl.pallas_call(wrapped, out_shape=[jax.ShapeDtypeStruct(o[0], o[1]) for o...]
    unnamed x94 -> x90, local copies, waits for them, and re-layouts: 7.22 us -> 6.51 us
  transfers between devices with their start and end apart: 61 -> 61, of which waited for: 30 -> 24; matrix products, arithmetic and copies ran while one was open for 9% -> 8% of each run, Pallas kernels for 20% -> 23%
where the time goes in v1:
time: 250 us; the launch traced here: 249 us
  waiting for transfers between devices  78.4 us (31%)
  Pallas kernels  74.6 us (30%)
  starting transfers between devices  66.2 us (26%)
  local copies, waits for them, and re-layouts  16.7 us (7%)
  other arithmetic  11.8 us (5%)
    ppermute x61, waiting for transfers between devices, swap(): return lax.ppermute(value, axis, [(i, i ^ bit) for i in range(size)])  78.4 us
    pallas_call x13, Pallas kernels, launch(): pl.pallas_call(wrapped, out_shape=[jax.ShapeDtypeStruct(o[0], o[1]) for o...  74.6 us
    ppermute x61, starting transfers between devices, swap(): return lax.ppermute(value, axis, [(i, i ^ bit) for i in range(size)])  66.2 us
    unnamed x90, local copies, waits for them, and re-layouts  6.51 us
  transfers between devices with their start and end apart: 61, of which 24 were waited for; matrix products, arithmetic and copies ran while one was open for 8% of the time, Pallas kernels for 23%

profile of v1, /device:TPU:0, one launch (start us, length us, event | category | flops | bytes accessed | tf_op | source)
XLA Modules:
  0.0 249.3 jit_solution(3530301450399277353)
XLA Ops:
  0.7 4.2 %shard_map.203 = (bf16[240,1600]{1,0:T(8,128)(2,1)}, bf16[4,128,256]{2,1,0:T(8,128)(2,1)}, bf16[4,128,256]{2,1,0:T(8,128)(2,1)}, f32[2,128,960]{2,1,0:T(8,128)}) custom-call(f32[960,128]{1,0:T(8,128)} %bitcast.166, f32[960,128]{1,0:T(8,128)} %bitcast.167, f32[1,960]{1,0:T(1,128)} %refs_7_.1, bf16[240,960]{1,0:T(8,128)(2,1)} %bitcast.168, ...), custom_call_target="tpu_custom_call" | custom-call | tf_op jit(solution)/shard_map/pallas_call | solution.py:190
  9.1 5.6 %shard_map.204 = (bf16[3,240,640]{2,1,0:T(8,128)(2,1)}, bf16[3,240,640]{2,1,0:T(8,128)(2,1)}, bf16[2,3,240,640]{3,2,1,0:T(8,128)(2,1)}) custom-call(s32[1]{0:T(128)} %bitcast.refs_0_, bf16[240,2560]{1,0:T(8,128)(2,1)} %bitcast.161, bf16[240,2560]{1,0:T(8,128)(2,1)} %bitcast.162, bf16[240,2560]{1,0:T(8,128)(2,1)} %bitcast.163), custom_call_target="tpu_custom_call" | custom-call | tf_op jit(solution)/shard_map/pallas_call | solution.py:190
  16.6 9.3 %collective-permute-done.refs_6_.refs_11_ = bf16[240,1600]{1,0:T(8,128)(2,1)S(1)} collective-permute-done((bf16[240,1600]{1,0:T(8,128)(2,1)}, bf16[240,1600]{1,0:T(8,128)(2,1)S(1)}, u32[]{:S(2)}, u32[]{:S(2)}) %collective-permute-start) | collective-permute-done | bytes 768032 | tf_op jit(solution)/shard_map/ppermute | solution.py:37
  29.2 4.3 %shard_map.205 = (bf16[128,960]{1,0:T(8,128)(2,1)}, bf16[128,640]{1,0:T(8,128)(2,1)}) custom-call(s32[1]{0:T(128)} %bitcast.refs_0_, bf16[4,128,256]{2,1,0:T(8,128)(2,1)} %get-tuple-element.195.refs_1_.refs_6_, f32[128,128]{1,0:T(8,128)} %pad_maximum_fusion.2.refs_2_.refs_13_.refs_3_, f32[128,128]{1,0:T(8,128)} %pad_maximum_fusion.3.refs_3_.refs_14_.refs_4_, ...), custom_call_target="tpu_custom_call" | custom-call | tf_op jit(solution)/shard_map/pallas_call | solution.py:190
  33.6 6.1 %collective-permute-done.11.refs_17_.refs_25_ = bf16[960,240]{1,0:T(8,128)(2,1)S(1)} collective-permute-done((bf16[960,240]{1,0:T(8,128)(2,1)S(1)}, bf16[960,240]{1,0:T(8,128)(2,1)S(1)}, u32[]{:S(2)}, u32[]{:S(2)}) %collective-permute-start.11) | collective-permute-done | bytes 460832 | tf_op jit(solution)/shard_map/ppermute | solution.py:37
  45.0 3.2 %collective-permute-done.3.refs_8_.refs_16_ = bf16[128,640]{1,0:T(8,128)(2,1)S(1)} collective-permute-done((bf16[128,640]{1,0:T(8,128)(2,1)}, bf16[128,640]{1,0:T(8,128)(2,1)S(1)}, u32[]{:S(2)}, u32[]{:S(2)}) %collective-permute-start.3) | collective-permute-done | bytes 163872 | tf_op jit(solution)/shard_map/ppermute | solution.py:37
  50.8 7.3 %collective-permute-done.5.refs_11_.refs_19_ = bf16[128,640]{1,0:T(8,128)(2,1)S(1)} collective-permute-done((bf16[128,640]{1,0:T(8,128)(2,1)}, bf16[128,640]{1,0:T(8,128)(2,1)S(1)}, u32[]{:S(2)}, u32[]{:S(2)}) %collective-permute-start.5) | collective-permute-done | bytes 163872 | tf_op jit(solution)/shard_map/ppermute | solution.py:37
  61.1 4.2 %collective-permute-done.8.refs_10_.refs_18_ = bf16[128,640]{1,0:T(8,128)(2,1)S(1)} collective-permute-done((bf16[128,640]{1,0:T(8,128)(2,1)S(1)}, bf16[128,640]{1,0:T(8,128)(2,1)S(1)}, u32[]{:S(2)}, u32[]{:S(2)}) %collective-permute-start.8) | collective-permute-done | bytes 163872 | tf_op jit(solution)/shard_map/ppermute | solution.py:37
  75.1 8.7 %shard_map.206 = (bf16[128,960]{1,0:T(8,128)(2,1)}, f32[5,384]{1,0:T(8,128)}, f32[128,960]{1,0:T(8,128)}, bf16[4,128,256]{2,1,0:T(8,128)(2,1)}) custom-call(s32[1]{0:T(128)} %bitcast.refs_0_, bf16[128,960]{1,0:T(8,128)(2,1)} %get-tuple-element.142.refs_1_.refs_8_, s32[512,1]{1,0:T(8,128)} %copy.55.refs_2_.refs_10_, s32[512,1]{1,0:T(8,128)} %copy.56.refs_3_.refs_11_, ...), custom_call_target="tpu_custom_call" | custom-call | tf_op jit(solution)/shard_map/pallas_call | solution.py:190
  84.3 4.4 %collective-permute-done.17.refs_7_.refs_4_ = bf16[4,128,256]{2,1,0:T(8,128)(2,1)} collective-permute-done((bf16[4,128,256]{2,1,0:T(8,128)(2,1)S(1)}, bf16[4,128,256]{2,1,0:T(8,128)(2,1)}, u32[]{:S(2)}, u32[]{:S(2)}) %collective-permute-start.17) | collective-permute-done | bytes 262176 | tf_op jit(solution)/shard_map/ppermute | solution.py:37
  88.7 4.2 %collective-permute-done.15.refs_3_.refs_4_ = bf16[4,128,256]{2,1,0:T(8,128)(2,1)S(1)} collective-permute-done((bf16[4,128,256]{2,1,0:T(8,128)(2,1)}, bf16[4,128,256]{2,1,0:T(8,128)(2,1)S(1)}, u32[]{:S(2)}, u32[]{:S(2)}) %collective-permute-start.15) | collective-permute-done | bytes 262176 | tf_op jit(solution)/shard_map/ppermute | solution.py:37
  98.7 9.7 %shard_map.207 = (bf16[2,4,128,256]{3,2,1,0:T(8,128)(2,1)}, bf16[2,4,128,256]{3,2,1,0:T(8,128)(2,1)}, bf16[512,640]{1,0:T(8,128)(2,1)}, bf16[512,640]{1,0:T(8,128)(2,1)}, bf16[512,640]{1,0:T(8,128)(2,1)}) custom-call(s32[1]{0:T(128)} %bitcast.refs_0_, bf16[4,128,256]{2,1,0:T(8,128)(2,1)} %get-tuple-element.164.refs_1_.refs_2_, ...), custom_call_target="tpu_custom_call" | custom-call | tf_op jit(solution)/shard_map/pallas_call | solution.py:190
  111.8 3.4 %shard_map.208 = (bf16[4,320,240]{2,1,0:T(8,128)(2,1)}, bf16[4,320,240]{2,1,0:T(8,128)(2,1)}) custom-call(s32[1]{0:T(128)} %bitcast.refs_0_, s32[1]{0:T(128)} %bitcast.17.refs_1_, bf16[4,128,256]{2,1,0:T(8,128)(2,1)} %get-tuple-element.168.refs_5_.refs_2_, bf16[4,128,256]{2,1,0:T(8,128)(2,1)} %copy-done.23, ...), custom_call_target="tpu_custom_call" | custom-call | tf_op jit(solution)/shard_map/pallas_call | solution.py:190
  118.5 4.4 %shard_map.209 = (bf16[4,320,240]{2,1,0:T(8,128)(2,1)}, bf16[4,320,240]{2,1,0:T(8,128)(2,1)}, bf16[4,320,240]{2,1,0:T(8,128)(2,1)}, bf16[4,320,240]{2,1,0:T(8,128)(2,1)}) custom-call(s32[1]{0:T(128)} %bitcast.refs_0_, s32[1]{0:T(128)} %bitcast.17.refs_1_, bf16[4,128,256]{2,1,0:T(8,128)(2,1)} %get-tuple-element.164.refs_1_.refs_2_, ...), custom_call_target="tpu_custom_call" | custom-call | tf_op jit(solution)/shard_map/pallas_call | solution.py:190
  126.6 12.1 %shard_map.210 = (f32[128,960]{1,0:T(8,128)}, bf16[3,4,128,256]{3,2,1,0:T(8,128)(2,1)}, f32[1,960]{1,0:T(1,128)}, bf16[4,128,640]{2,1,0:T(8,128)(2,1)}, bf16[4,128,640]{2,1,0:T(8,128)(2,1)}) custom-call(s32[1]{0:T(128)} %bitcast.refs_0_, bf16[2,4,128,256]{3,2,1,0:T(8,128)(2,1)} %get-tuple-element.173.refs_1_, bf16[2,4,128,256]{3,2,1,0:T(8,128)(2,1)} %copy-done.13, ...), custom_call_target="tpu_custom_call" | custom-call | tf_op jit(solution)/shard_map/pallas_call | solution.py:190
  140.6 5.5 %shard_map.211 = (bf16[2,4,128,256]{3,2,1,0:T(8,128)(2,1)}, bf16[2,4,128,256]{3,2,1,0:T(8,128)(2,1)}) custom-call(s32[1]{0:T(128)} %bitcast.refs_0_, bf16[3,240,640]{2,1,0:T(8,128)(2,1)} %get-tuple-element.170.refs_9_.refs_1_, bf16[3,240,640]{2,1,0:T(8,128)(2,1)} %copy-done.1, bf16[2,3,240,640]{3,2,1,0:T(8,128)(2,1)} %copy-done, ...), custom_call_target="tpu_custom_call" | custom-call | tf_op jit(solution)/shard_map/pallas_call | solution.py:190
  149.1 8.2 %collective-permute-done.27.refs_4_ = bf16[3,4,128,256]{3,2,1,0:T(8,128)(2,1)} collective-permute-done((bf16[3,4,128,256]{3,2,1,0:T(8,128)(2,1)}, bf16[3,4,128,256]{3,2,1,0:T(8,128)(2,1)}, u32[]{:S(2)}, u32[]{:S(2)}) %collective-permute-start.27) | collective-permute-done | bytes 786464 | tf_op jit(solution)/shard_map/ppermute | solution.py:37
  162.9 4.0 %shard_map.212 = (bf16[4,240,240]{2,1,0:T(8,128)(2,1)}, bf16[4,240,240]{2,1,0:T(8,128)(2,1)}) custom-call(s32[1]{0:T(128)} %bitcast.refs_0_, s32[1]{0:T(128)} %bitcast.17.refs_1_, bf16[3,4,128,256]{3,2,1,0:T(8,128)(2,1)} %get-tuple-element.194.refs_2_.refs_5_, bf16[3,4,128,256]{3,2,1,0:T(8,128)(2,1)} %collective-permute-done.28.refs_3_, ...), custom_call_target="tpu_custom_call" | custom-call | tf_op jit(solution)/shard_map/pallas_call | solution.py:190
  177.1 4.8 %collective-permute-done.35.refs_2_ = bf16[1,128,640]{2,1,0:T(8,128)(2,1)S(1)} collective-permute-done((bf16[1,128,640]{2,1,0:T(8,128)(2,1)S(1)}, bf16[1,128,640]{2,1,0:T(8,128)(2,1)S(1)}, u32[]{:S(2)}, u32[]{:S(2)}) %collective-permute-start.35) | collective-permute-done | bytes 163872 | tf_op jit(solution)/shard_map/ppermute | solution.py:37
  182.5 6.7 %shard_map.213 = (bf16[128,640]{1,0:T(8,128)(2,1)}, f32[960,128]{1,0:T(8,128)}, f32[1,960]{1,0:T(1,128)}) custom-call(s32[1]{0:T(128)} %bitcast.refs_0_, bf16[1,128,640]{2,1,0:T(8,128)(2,1)} %get-tuple-element.300.refs_1_, bf16[1,128,640]{2,1,0:T(8,128)(2,1)} %copy-done.38, f32[128,128]{1,0:T(8,128)} %pad_maximum_fusion.2.refs_2_.refs_13_.refs_3_, ...), custom_call_target="tpu_custom_call" | custom-call | tf_op jit(solution)/shard_map/pallas_call | solution.py:190
  198.0 3.4 %collective-permute-start.55 = (bf16[1,320,240]{2,1,0:T(8,128)(2,1)}, bf16[1,320,240]{2,1,0:T(8,128)(2,1)}, u32[]{:S(2)}, u32[]{:S(2)}) collective-permute-start(bf16[1,320,240]{2,1,0:T(8,128)(2,1)} %constant_dynamic-slice_fusion.6), channel_id=1, source_target_pairs={{0,16},{4,20},{8,24},{12,28},{16,0},{20,4},{24,8},{28,12},{1,17},{... | collective-permute-start | bytes 460808 | tf_op jit(solution)/shard_map/ppermute | solution.py:37
  201.5 3.5 %shard_map.214 = (bf16[4,80,240]{2,1,0:T(8,128)(2,1)}, bf16[4,80,240]{2,1,0:T(8,128)(2,1)}) custom-call(s32[1]{0:T(128)} %bitcast.refs_0_, s32[1]{0:T(128)} %bitcast.17.refs_1_, bf16[128,640]{1,0:T(8,128)(2,1)} %get-tuple-element.215.refs_2_, bf16[128,640]{1,0:T(8,128)(2,1)} %collective-permute-done.41.refs_3_, bf16[128,640]{1,0:T(8,128)(2,1)} %copy-done.39, ...), custom_call_target="tpu_custom_call" | custom-call | tf_op jit(solution)/shard_map/pallas_call | solution.py:190
  205.8 3.5 %collective-permute-done.40 = bf16[2,320,240]{2,1,0:T(8,128)(2,1)} collective-permute-done((bf16[2,320,240]{2,1,0:T(8,128)(2,1)}, bf16[2,320,240]{2,1,0:T(8,128)(2,1)}, u32[]{:S(2)}, u32[]{:S(2)}) %collective-permute-start.40) | collective-permute-done | bytes 307232 | tf_op jit(solution)/shard_map/ppermute | solution.py:37
  214.3 3.7 %collective-permute-start.56 = (bf16[1,320,240]{2,1,0:T(8,128)(2,1)S(1)}, bf16[1,320,240]{2,1,0:T(8,128)(2,1)S(1)}, u32[]{:S(2)}, u32[]{:S(2)}) collective-permute-start(bf16[1,320,240]{2,1,0:T(8,128)(2,1)S(1)} %constant_dynamic-slice_fusion.5), channel_id=1, source_target_pairs={{0,16},{4,20},{8,24},{12,28},{16,0},{20,4},{24,8},{28,12},{1,17},{... | collective-permute-start | bytes 460808 | tf_op jit(solution)/shard_map/ppermute | solution.py:37
  (266 shorter events, 113.6 us)
Async XLA Ops:
  4.9 21.0 %collective-permute-start = (bf16[240,1600]{1,0:T(8,128)(2,1)}, bf16[240,1600]{1,0:T(8,128)(2,1)S(1)}, u32[]{:S(2)}, u32[]{:S(2)}) collective-permute-start(bf16[240,1600]{1,0:T(8,128)(2,1)} %get-tuple-element.133.refs_4_.refs_9_), channel_id=1, source_target_pairs={{0,2},{1,3},{2,0},{3,1},{4,6},{5,7},{6,4},{7,5},{8,10},{9,11},{10,... | collective-permute-start | bytes 2304008 | tf_op jit(solution)/shard_map/ppermute | solution.py:37
  7.9 18.0 %collective-permute-start.1 = (bf16[240,1600]{1,0:T(8,128)(2,1)}, bf16[240,1600]{1,0:T(8,128)(2,1)S(1)}, u32[]{:S(2)}, u32[]{:S(2)}) collective-permute-start(bf16[240,1600]{1,0:T(8,128)(2,1)} %get-tuple-element.133.refs_4_.refs_9_), channel_id=1, source_target_pairs={{0,1},{1,0},{2,3},{3,2},{4,5},{5,4},{6,7},{7,6},{8,9},{9,8},{10,11... | collective-permute-start | bytes 2304008 | tf_op jit(solution)/shard_map/ppermute | solution.py:37
  26.0 13.6 %collective-permute-start.11 = (bf16[960,240]{1,0:T(8,128)(2,1)S(1)}, bf16[960,240]{1,0:T(8,128)(2,1)S(1)}, u32[]{:S(2)}, u32[]{:S(2)}) collective-permute-start(bf16[960,240]{1,0:T(8,128)(2,1)S(1)} %bitcast.159), channel_id=1, source_target_pairs={{0,2},{1,3},{2,0},{3,1},{4,6},{5,7},{6,4},{7,5},{8,10},{9,11},{10,... | collective-permute-start | bytes 1382408 | tf_op jit(solution)/shard_map/ppermute | solution.py:37
  39.6 53.2 %collective-permute-start.18 = (bf16[2,3,240,640]{3,2,1,0:T(8,128)(2,1)}, bf16[2,3,240,640]{3,2,1,0:T(8,128)(2,1)S(1)}, u32[]{:S(2)}, u32[]{:S(2)}) collective-permute-start(bf16[2,3,240,640]{3,2,1,0:T(8,128)(2,1)} %get-tuple-element.167), channel_id=1, source_target_pairs={{0,2},{1,3},{2,0},{3,1},{4,6},{5,7},{6,4},{7,5},{8,10},{9,11},{10,... | collective-permute-start | bytes 5529608 | tf_op jit(solution)/shard_map/ppermute | solution.py:37
  41.4 16.7 %collective-permute-start.7 = (bf16[3,240,640]{2,1,0:T(8,128)(2,1)}, bf16[3,240,640]{2,1,0:T(8,128)(2,1)S(1)}, u32[]{:S(2)}, u32[]{:S(2)}) collective-permute-start(bf16[3,240,640]{2,1,0:T(8,128)(2,1)} %get-tuple-element.151), channel_id=1, source_target_pairs={{0,1},{1,0},{2,3},{3,2},{4,5},{5,4},{6,7},{7,6},{8,9},{9,8},{10,11... | collective-permute-start | bytes 2764808 | tf_op jit(solution)/shard_map/ppermute | solution.py:37
  41.4 16.7 %collective-permute-start.6 = (bf16[960,240]{1,0:T(8,128)(2,1)S(1)}, bf16[960,240]{1,0:T(8,128)(2,1)S(1)}, u32[]{:S(2)}, u32[]{:S(2)}) collective-permute-start(bf16[960,240]{1,0:T(8,128)(2,1)S(1)} %bitcast.160), channel_id=1, source_target_pairs={{0,1},{1,0},{2,3},{3,2},{4,5},{5,4},{6,7},{7,6},{8,9},{9,8},{10,11... | collective-permute-start | bytes 1382408 | tf_op jit(solution)/shard_map/ppermute | solution.py:37
  72.2 16.5 %collective-permute-start.17 = (bf16[4,128,256]{2,1,0:T(8,128)(2,1)S(1)}, bf16[4,128,256]{2,1,0:T(8,128)(2,1)}, u32[]{:S(2)}, u32[]{:S(2)}) collective-permute-start(bf16[4,128,256]{2,1,0:T(8,128)(2,1)S(1)} %copy-done.19), channel_id=1, source_target_pairs={{0,2},{1,3},{2,0},{3,1},{4,6},{5,7},{6,4},{7,5},{8,10},{9,11},{10,... | collective-permute-start | bytes 786440 | tf_op jit(solution)/shard_map/ppermute | solution.py:37
  115.2 24.3 %collective-permute-start.25 = (bf16[4,320,240]{2,1,0:T(8,128)(2,1)}, bf16[4,320,240]{2,1,0:T(8,128)(2,1)}, u32[]{:S(2)}, u32[]{:S(2)}) collective-permute-start(bf16[4,320,240]{2,1,0:T(8,128)(2,1)} %get-tuple-element.180), channel_id=1, source_target_pairs={{0,4},{4,0},{8,12},{12,8},{16,20},{20,16},{24,28},{28,24},{1,5},{5... | collective-permute-start | bytes 1843208 | tf_op jit(solution)/shard_map/ppermute | solution.py:37
  125.1 14.4 %collective-permute-start.24 = (bf16[4,128,256]{2,1,0:T(8,128)(2,1)S(1)}, bf16[4,128,256]{2,1,0:T(8,128)(2,1)S(1)}, u32[]{:S(2)}, u32[]{:S(2)}) collective-permute-start(bf16[4,128,256]{2,1,0:T(8,128)(2,1)S(1)} %copy-done.6), channel_id=1, source_target_pairs={{0,2},{1,3},{2,0},{3,1},{4,6},{5,7},{6,4},{7,5},{8,10},{9,11},{10,... | collective-permute-start | bytes 786440 | tf_op jit(solution)/shard_map/ppermute | solution.py:37
  138.7 18.6 %collective-permute-start.27 = (bf16[3,4,128,256]{3,2,1,0:T(8,128)(2,1)}, bf16[3,4,128,256]{3,2,1,0:T(8,128)(2,1)}, u32[]{:S(2)}, u32[]{:S(2)}) collective-permute-start(bf16[3,4,128,256]{3,2,1,0:T(8,128)(2,1)} %get-tuple-element.194.refs_2_.refs_5_), channel_id=1, source_target_pairs={{0,2},{1,3},{2,0},{3,1},{4,6},{5,7},{6,4},{7,5},{8,10},{9,11},{10,... | collective-permute-start | bytes 2359304 | tf_op jit(solution)/shard_map/ppermute | solution.py:37
  139.5 17.9 %collective-permute-start.28 = (bf16[3,4,128,256]{3,2,1,0:T(8,128)(2,1)}, bf16[3,4,128,256]{3,2,1,0:T(8,128)(2,1)}, u32[]{:S(2)}, u32[]{:S(2)}) collective-permute-start(bf16[3,4,128,256]{3,2,1,0:T(8,128)(2,1)} %get-tuple-element.194.refs_2_.refs_5_), channel_id=1, source_target_pairs={{0,1},{1,0},{2,3},{3,2},{4,5},{5,4},{6,7},{7,6},{8,9},{9,8},{10,11... | collective-permute-start | bytes 2359304 | tf_op jit(solution)/shard_map/ppermute | solution.py:37
  139.5 17.9 %collective-permute-start.26 = (bf16[4,128,640]{2,1,0:T(8,128)(2,1)}, bf16[4,128,640]{2,1,0:T(8,128)(2,1)}, u32[]{:S(2)}, u32[]{:S(2)}) collective-permute-start(bf16[4,128,640]{2,1,0:T(8,128)(2,1)} %get-tuple-element.193), channel_id=1, source_target_pairs={{0,4},{4,0},{8,12},{12,8},{16,20},{20,16},{24,28},{28,24},{1,5},{5... | collective-permute-start | bytes 1966088 | tf_op jit(solution)/shard_map/ppermute | solution.py:37
  161.1 29.8 %collective-permute-start.38 = (bf16[4,320,240]{2,1,0:T(8,128)(2,1)}, bf16[4,320,240]{2,1,0:T(8,128)(2,1)S(1)}, u32[]{:S(2)}, u32[]{:S(2)}) collective-permute-start(bf16[4,320,240]{2,1,0:T(8,128)(2,1)} %get-tuple-element.219), channel_id=1, source_target_pairs={{0,4},{4,0},{8,12},{12,8},{16,20},{20,16},{24,28},{28,24},{1,5},{5... | collective-permute-start | bytes 1843208 | tf_op jit(solution)/shard_map/ppermute | solution.py:37
  175.0 21.5 %collective-permute-start.32 = (bf16[4,320,240]{2,1,0:T(8,128)(2,1)}, bf16[4,320,240]{2,1,0:T(8,128)(2,1)S(1)}, u32[]{:S(2)}, u32[]{:S(2)}) collective-permute-start(bf16[4,320,240]{2,1,0:T(8,128)(2,1)} %get-tuple-element.202), channel_id=1, source_target_pairs={{0,4},{4,0},{8,12},{12,8},{16,20},{20,16},{24,28},{28,24},{1,5},{5... | collective-permute-start | bytes 1843208 | tf_op jit(solution)/shard_map/ppermute | solution.py:37
  175.5 29.5 %collective-permute-start.46 = (bf16[4,240,240]{2,1,0:T(8,128)(2,1)}, bf16[4,240,240]{2,1,0:T(8,128)(2,1)S(1)}, u32[]{:S(2)}, u32[]{:S(2)}) collective-permute-start(bf16[4,240,240]{2,1,0:T(8,128)(2,1)} %get-tuple-element.236), channel_id=1, source_target_pairs={{0,4},{4,0},{8,12},{12,8},{16,20},{20,16},{24,28},{28,24},{1,5},{5... | collective-permute-start | bytes 1382408 | tf_op jit(solution)/shard_map/ppermute | solution.py:37
  195.0 14.3 %collective-permute-start.40 = (bf16[2,320,240]{2,1,0:T(8,128)(2,1)}, bf16[2,320,240]{2,1,0:T(8,128)(2,1)}, u32[]{:S(2)}, u32[]{:S(2)}) collective-permute-start(bf16[2,320,240]{2,1,0:T(8,128)(2,1)} %dynamic-slice_bitcast_fusion.1), channel_id=1, source_target_pairs={{0,8},{4,12},{8,0},{12,4},{16,24},{20,28},{24,16},{28,20},{1,9},{5... | collective-permute-start | bytes 921608 | tf_op jit(solution)/shard_map/ppermute | solution.py:37
  198.0 12.8 %collective-permute-start.55 = (bf16[1,320,240]{2,1,0:T(8,128)(2,1)}, bf16[1,320,240]{2,1,0:T(8,128)(2,1)}, u32[]{:S(2)}, u32[]{:S(2)}) collective-permute-start(bf16[1,320,240]{2,1,0:T(8,128)(2,1)} %constant_dynamic-slice_fusion.6), channel_id=1, source_target_pairs={{0,16},{4,20},{8,24},{12,28},{16,0},{20,4},{24,8},{28,12},{1,17},{... | collective-permute-start | bytes 460808 | tf_op jit(solution)/shard_map/ppermute | solution.py:37
  201.4 12.9 %collective-permute-start.44 = (bf16[2,4,128,256]{3,2,1,0:T(8,128)(2,1)}, bf16[2,4,128,256]{3,2,1,0:T(8,128)(2,1)S(1)}, u32[]{:S(2)}, u32[]{:S(2)}) collective-permute-start(bf16[2,4,128,256]{3,2,1,0:T(8,128)(2,1)} %get-tuple-element.231), channel_id=1, source_target_pairs={{0,1},{1,0},{2,3},{3,2},{4,5},{5,4},{6,7},{7,6},{8,9},{9,8},{10,11... | collective-permute-start | bytes 1572872 | tf_op jit(solution)/shard_map/ppermute | solution.py:37
  201.5 16.6 %collective-permute-start.39 = (bf16[2,320,240]{2,1,0:T(8,128)(2,1)}, bf16[2,320,240]{2,1,0:T(8,128)(2,1)S(1)}, u32[]{:S(2)}, u32[]{:S(2)}) collective-permute-start(bf16[2,320,240]{2,1,0:T(8,128)(2,1)} %dynamic-slice_bitcast_fusion), channel_id=1, source_target_pairs={{0,8},{4,12},{8,0},{12,4},{16,24},{20,28},{24,16},{28,20},{1,9},{5... | collective-permute-start | bytes 921608 | tf_op jit(solution)/shard_map/ppermute | solution.py:37
  205.1 14.2 %collective-permute-start.47 = (bf16[4,80,240]{2,1,0:T(8,128)(2,1)}, bf16[4,80,240]{2,1,0:T(8,128)(2,1)}, u32[]{:S(2)}, u32[]{:S(2)}) collective-permute-start(bf16[4,80,240]{2,1,0:T(8,128)(2,1)} %get-tuple-element.225), channel_id=1, source_target_pairs={{0,4},{4,0},{8,12},{12,8},{16,20},{20,16},{24,28},{28,24},{1,5},{5... | collective-permute-start | bytes 460808 | tf_op jit(solution)/shard_map/ppermute | solution.py:37
  210.1 12.5 %collective-permute-start.49 = (f32[2,960]{1,0:T(2,128)S(1)}, f32[2,960]{1,0:T(2,128)S(1)}, u32[]{:S(2)}, u32[]{:S(2)}) collective-permute-start(f32[2,960]{1,0:T(2,128)S(1)} %add.208), channel_id=1, source_target_pairs={{0,4},{4,0},{8,12},{12,8},{16,20},{20,16},{24,28},{28,24},{1,5},{5... | collective-permute-start | bytes 23048 | tf_op jit(solution)/shard_map/ppermute | solution.py:37
  210.8 20.3 %collective-permute-start.51 = (bf16[2,240,240]{1,2,0:T(8,128)(2,1)}, bf16[2,240,240]{1,2,0:T(8,128)(2,1)S(1)}, u32[]{:S(2)}, u32[]{:S(2)}) collective-permute-start(bf16[2,240,240]{1,2,0:T(8,128)(2,1)} %bitcast.170), channel_id=1, source_target_pairs={{0,8},{4,12},{8,0},{12,4},{16,24},{20,28},{24,16},{28,20},{1,9},{5... | collective-permute-start | bytes 691208 | tf_op jit(solution)/shard_map/ppermute | solution.py:37
  218.1 19.1 %collective-permute-start.45 = (bf16[4,128,256]{2,1,0:T(8,128)(2,1)S(1)}, bf16[4,128,256]{2,1,0:T(8,128)(2,1)S(1)}, u32[]{:S(2)}, u32[]{:S(2)}) collective-permute-start(bf16[4,128,256]{2,1,0:T(8,128)(2,1)S(1)} %fusion.7), channel_id=1, source_target_pairs={{0,2},{1,3},{2,0},{3,1},{4,6},{5,7},{6,4},{7,5},{8,10},{9,11},{10,... | collective-permute-start | bytes 786440 | tf_op jit(solution)/shard_map/ppermute | solution.py:37
  219.3 21.2 %collective-permute-start.57 = (bf16[1,320,240]{2,1,0:T(8,128)(2,1)S(1)}, bf16[1,320,240]{2,1,0:T(8,128)(2,1)S(1)}, u32[]{:S(2)}, u32[]{:S(2)}) collective-permute-start(bf16[1,320,240]{2,1,0:T(8,128)(2,1)S(1)} %constant_dynamic-slice_fusion.4), channel_id=1, source_target_pairs={{0,16},{4,20},{8,24},{12,28},{16,0},{20,4},{24,8},{28,12},{1,17},{... | collective-permute-start | bytes 460808 | tf_op jit(solution)/shard_map/ppermute | solution.py:37
  (81 other events, 606.0 us)
